TPU v7x, 32 devices: a whole 2x2x4 slice. The times are simulated.
32 devices in a mesh: tm: 4 (over y, x), space: 8 (over z, core).
Axes of the slice: x: 2, y: 2, z: 4, core: 2. Of those that a mesh axis runs over, the one named last changes fastest.
Arguments:
- vectors: float32 [4, 2, 3, 64, 2048], P('tm', None, None, None, 'space'), may hold values from -6 to 6
- perambulators: float32 [4, 16, 2, 4096], P('tm'), may hold values from -0.75 to 0.75
- shift_steps: int32 [4], P('tm'), may hold values from 1 to 3, as said below
- spin_choice: int32 [4, 3], replicated, may hold values from 0 to 15
Outputs:
- elementals: float32 [4, 64, 2, 4096], P('tm', 'space')
- correlator: float32 [4, 4, 2], P('tm')
Inputs may be any that keep to these rules, and one draw needn't show every extreme that they name: `shift_steps`: every distance from 1 to 3 is taken by at least one source timeslice. `spin_choice`: each entry is alpha 4 + beta for a pair of spin indices.
All inputs are finite; a program needn't handle non-finite values.
Results may differ from a plain program's by a relative error of at most 0.0003.
Values sent between devices are 32-bit elements; how exact they have to be, the bound alone decides.
A program may use at most 64 MiB of HBM per device.

v0:
```python
import functools
import math

import jax
import jax.numpy as jnp
from jax import lax
from jax.experimental import pallas as pl
from jax.experimental.pallas import tpu as pltpu
from jax.sharding import PartitionSpec as P

MESH = pl.DeviceIdType.MESH
VM = pl.BlockSpec(memory_space=pltpu.VMEM)
NT_DIMS = (((1,), (1,)), ((), ()))


def halves(x):
    top = x.astype(jnp.bfloat16)
    return top, (x - top.astype(jnp.float32)).astype(jnp.bfloat16)


def at_space(index):
    return (lax.axis_index("tm"), index)


def elementals_kernel(
    n, times, scale, corr_scale, v_ref, mats_ref, shift_ref, spin_ref, out_ref, corr_ref,
    own_ref, full_ref, sink_ref, lead, d_hi, d_lo, keep, give, pair_in, chip_in,
    right_hi, right_lo, half_hi, half_lo, weight, mixed_rows, chosen, board, spin_mats, tile_ref, box,
    pair_send, pair_recv, chip_send, chip_recv,
    own_send, own_recv, fwd_send, fwd_recv, tm_send, tm_recv,
    sum_send, sum_recv,
):
    me = lax.axis_index("space")
    tm = lax.axis_index("tm")
    chips = n // 2
    chip = me // 2
    core = me % 2
    mate = chip * 2 + 1 - core
    nvec = v_ref.shape[2]
    sites = v_ref.shape[3]
    own = nvec // n
    half = nvec // 2
    lanes = 2 * nvec
    group = 16 // own

    barrier = pltpu.get_barrier_semaphore()
    for r in range(1, n):
        pl.semaphore_signal(barrier, inc=1, device_id=(tm, (me + r) % n), device_id_type=MESH)
    for r in range(1, times):
        pl.semaphore_signal(
            barrier, inc=1, device_id=((tm + r) % times, me), device_id_type=MESH
        )

    for kind in range(2):
        for a in range(3):
            re = v_ref[0, a]
            im = v_ref[1, a]
            if kind == 1:
                re = jnp.concatenate([re[half:], re[:half]], axis=0)
                im = jnp.concatenate([im[half:], im[:half]], axis=0)
            re_hi, re_lo = halves(re)
            im_hi, im_lo = halves(im)
            first = pl.ds(a * sites, sites)
            second = pl.ds((3 + a) * sites, sites)
            lead[kind, 0:nvec, first] = re_hi
            lead[kind, 0:nvec, second] = -im_hi
            lead[kind, nvec:lanes, first] = im_hi
            lead[kind, nvec:lanes, second] = re_hi
            lead[kind, lanes:lanes + nvec, first] = re_lo
            lead[kind, lanes:lanes + nvec, second] = -im_lo
            lead[kind, lanes + nvec:2 * lanes, first] = im_lo
            lead[kind, lanes + nvec:2 * lanes, second] = re_lo

    rows = half * own
    row_of = lax.broadcasted_iota(jnp.int32, (rows, lanes), 0) // own
    place = lax.broadcasted_iota(jnp.int32, (rows, lanes), 1) % nvec
    later = jnp.logical_or(place < half, place - half < row_of)

    def block(dest, out_ref):
        start = pl.multiple_of(dest * own, own)

        def rows_of(c, a):
            if own % 8 == 0:
                return v_ref[c, a, pl.ds(start, own), :]
            single = [v_ref[c, a, pl.ds(start + r, 1), :] for r in range(own)]
            return jnp.concatenate(single, axis=0)

        mine = [[rows_of(c, a) for a in range(3)] for c in range(2)]

        def fill(step, carry):
            base = step * group
            for side in range(2):
                got = []
                for g in range(group):
                    k = side * half + base + g
                    other = [[v_ref[c, a, pl.ds(k, 1), :] for a in range(3)] for c in range(2)]
                    cross = []
                    for a in range(3):
                        b, d = (a + 1) % 3, (a + 2) % 3
                        cross.append(
                            mine[0][b] * other[0][d] - mine[1][b] * other[1][d]
                            - (mine[0][d] * other[0][b] - mine[1][d] * other[1][b])
                        )
                    for a in range(3):
                        b, d = (a + 1) % 3, (a + 2) % 3
                        cross.append(
                            mine[0][b] * other[1][d] + mine[1][b] * other[0][d]
                            - (mine[0][d] * other[1][b] + mine[1][d] * other[0][b])
                        )
                    got.append(cross)
                at = pl.ds(pl.multiple_of(base * own, 16), 16)
                for m in range(6):
                    hi, lo = halves(jnp.concatenate([g[m] for g in got], axis=0))
                    d_hi[side, at, m * sites:(m + 1) * sites] = hi
                    d_lo[side, at, m * sites:(m + 1) * sites] = lo
            return carry

        lax.fori_loop(0, half // group, fill, 0)
        sums = []
        for side in range(2):
            kind = 1 - side
            both = lax.dot_general(
                d_hi[side], lead[kind], NT_DIMS, preferred_element_type=jnp.float32
            )
            rest = lax.dot_general(
                d_lo[side], lead[kind, 0:lanes], NT_DIMS, preferred_element_type=jnp.float32
            )
            sums.append(both[:, :lanes] + (both[:, lanes:] + rest))
        out_ref[...] = jnp.where(later, sums[1], sums[0])

    def pair_copy(s):
        return pltpu.make_async_remote_copy(
            give.at[s], pair_in.at[s], pair_send.at[s], pair_recv.at[s],
            device_id=(tm, mate), device_id_type=MESH,
        )

    def chip_copy(s):
        return pltpu.make_async_remote_copy(
            keep.at[s], chip_in.at[s], chip_send.at[s], chip_recv.at[s],
            device_id=(tm, (chip + 1 + s) % chips * 2 + core), device_id_type=MESH,
        )

    def give_block(s):
        block((chip + 1 + s) % chips * 2 + 1 - core, give.at[s])

    def one_chip(s, carry):
        pair_copy(s).start()
        block((chip + 1 + s) % chips * 2 + core, keep.at[s])
        pair_copy(s).wait_recv()
        keep[s] = keep[s] + pair_in[s]

        @pl.when(s < chips - 1)
        def _():
            chip_copy(s).start()
            give_block(s + 1)

        return carry

    give_block(0)
    pl.semaphore_wait(barrier, n - 1 + times - 1)
    lax.fori_loop(0, chips, one_chip, 0)
    row = lax.broadcasted_iota(jnp.int32, (half, lanes), 0)
    lane = lax.broadcasted_iota(jnp.int32, (half, lanes), 1)
    spot = lane % nvec
    left = spot < half
    real = lane < nvec
    minus_plus = jnp.where(lax.broadcasted_iota(jnp.int32, (nvec, lanes), 1) < nvec, -1.0, 1.0)

    def weave(ref):
        even = ref[pl.ds(0, half, stride=2), :]
        odd = ref[pl.ds(1, half, stride=2), :]
        return (
            jnp.where(real, even, pltpu.roll(odd, nvec, 1)),
            jnp.where(real, pltpu.roll(even, nvec, 1), odd),
        )

    combos = spin_ref.shape[0]
    for s in range(combos):
        for q in range(3):
            board[...] = mats_ref[spin_ref[s, q]]
            even, odd = weave(board)
            spin_mats[s, q, pl.ds(0, half, stride=2), :] = even
            spin_mats[s, q, pl.ds(1, half, stride=2), :] = odd
    for s in range(combos):
        for q in range(2):
            spins = spin_mats[s, 2 * q]
            at = (s * 2 + q) * lanes
            top_hi, top_lo = halves(spins)
            low_hi, low_lo = halves(-minus_plus * pltpu.roll(spins, nvec, 1))
            right_hi[0:nvec, at:at + lanes] = top_hi
            right_lo[0:nvec, at:at + lanes] = top_lo
            right_hi[nvec:lanes, at:at + lanes] = low_hi
            right_lo[nvec:lanes, at:at + lanes] = low_lo

    total = keep[chips - 1]
    for s in range(chips - 1):
        chip_copy(s).wait_recv()
        total = total + chip_in[s]
    own_ref[...] = total * scale

    def tm_copy(r):
        return pltpu.make_async_remote_copy(
            own_ref, sink_ref.at[r - 1], tm_send.at[r - 1], tm_recv.at[r - 1],
            device_id=((tm + r) % times, me), device_id_type=MESH,
        )

    def own_copy(r):
        target = mate if r == 0 else (chip + r) % chips * 2 + core
        return pltpu.make_async_remote_copy(
            own_ref, full_ref.at[me], own_send.at[r], own_recv.at[r],
            device_id=(tm, target), device_id_type=MESH,
        )

    def forward(r):
        slot = (chip + chips - r) % chips * 2 + core
        return pltpu.make_async_remote_copy(
            full_ref.at[slot], full_ref.at[slot], fwd_send.at[r - 1], fwd_recv.at[r - 1],
            device_id=(tm, mate), device_id_type=MESH,
        )

    for r in range(1, times):
        tm_copy(r).start()
    for r in range(1, chips):
        own_copy(r).start()
    own_copy(0).start()
    full_ref[me] = own_ref[...]

    def dense(p):
        t = jnp.transpose(jnp.concatenate([p] * (lanes // half), axis=0))
        base = jnp.where(real, t[:half], t[nvec:nvec + half])
        mixed = jnp.where(real, t[half:nvec], t[nvec + half:])
        moved = pltpu.roll(p, lanes - half, 1)
        zero = jnp.zeros_like(p)
        upper = jnp.where(spot > row, moved, jnp.where(spot < row, -mixed, zero))
        lower = jnp.where(spot - half < row, p, jnp.where(spot - half > row, -mixed, zero))
        return jnp.where(left, upper, -base), jnp.where(left, p, lower)

    for j in range(own):
        top, bottom = dense(own_ref[pl.ds(j, half, stride=own), :])
        board[0:half, :] = -top
        board[half:nvec, :] = -bottom
        even, odd = weave(board)
        out_ref[j, pl.ds(0, half, stride=2), :] = even
        out_ref[j, pl.ds(1, half, stride=2), :] = odd

    def dot3(a_hi, a_lo, b_hi, b_lo):
        def dot(a, b):
            return jnp.dot(a, b, preferred_element_type=jnp.float32)

        return dot(a_hi, b_hi) + (dot(a_hi, b_lo) + dot(a_lo, b_hi))

    for r in range(1, times):
        tm_copy(r).wait_recv()
    chosen[...] = sink_ref[jnp.clip(times - 1 - shift_ref[0], 0, times - 2)]
    for j in range(own):
        top, bottom = dense(chosen[pl.ds(j, half, stride=own), :])
        hi, lo = halves(jnp.concatenate([top, bottom], axis=0))
        got = dot3(hi, lo, right_hi[...], right_lo[...])
        hi, lo = halves(got)
        for s in range(combos):
            for q in range(2):
                at = (s * 2 + q) * lanes
                where = (s, pl.ds(q * nvec, nvec), pl.ds(j * lanes, lanes))
                half_hi[where] = hi[:, at:at + lanes]
                half_lo[where] = lo[:, at:at + lanes]
    for r in range(1, chips):
        own_copy(r).wait_recv()
        forward(r).start()
    for s in range(combos):
        both = jnp.concatenate(
            [spin_mats[s, 2], spin_mats[s, 0]], axis=0
        )
        hi, lo = halves(jnp.transpose(both))
        got = dot3(hi, lo, half_hi[s], half_lo[s])
        for j in range(own):
            at = j * lanes
            whole = got[:nvec, at:at + lanes] + minus_plus * pltpu.roll(
                got[nvec:, at:at + lanes], nvec, 1
            )
            bent = jnp.where(
                jnp.logical_or(left, spot - half < row),
                whole[half:], pltpu.roll(whole[:half], half, 1),
            )
            weight[pl.ds((s * own + j) * half, half), :] = bent

    mid = []
    for s in range(combos):
        if own % 8 == 0:
            mid.append(spin_mats[s, 1, pl.ds(pl.multiple_of(me * own, own), own), :])
        else:
            for r in range(own):
                mid.append(spin_mats[s, 1, pl.ds(me * own + r, 1), :])
    mid = jnp.concatenate(mid, axis=0)
    count = combos * own
    mid = jnp.concatenate([mid[:, :nvec], pltpu.roll(mid, nvec, 1)[:, :nvec]], axis=0)
    mid_hi, mid_lo = halves(mid)
    own_copy(0).wait_recv()
    for r in range(1, chips):
        forward(r).wait_recv()
    sign = jnp.where(lax.broadcasted_iota(jnp.int32, (count, lanes), 1) < nvec, -1.0, 1.0)
    for k in range(half):
        pieces = [full_ref[d, k * own:(k + 1) * own, :] for d in range(n)]
        hi, lo = halves(jnp.concatenate(pieces, axis=0))
        got = dot3(mid_hi, mid_lo, hi, lo)
        mixed_rows[pl.ds(k * count, count), :] = got[:count] + sign * pltpu.roll(got[count:], nvec, 1)

    straight, crossed = [], []
    for s in range(combos):
        one = jnp.zeros((half, lanes), jnp.float32)
        two = jnp.zeros((half, lanes), jnp.float32)
        for j in range(own):
            at = s * own + j
            value = mixed_rows[pl.ds(at, half, stride=count), :]
            factor = weight[pl.ds(at * half, half), :]
            one = one + value * factor
            two = two + value * pltpu.roll(factor, nvec, 1)
        straight.append(jnp.sum(jnp.where(real, one, -one), axis=0, keepdims=True))
        crossed.append(jnp.sum(two, axis=0, keepdims=True))
    tile_ref[...] = jnp.concatenate(straight + crossed, axis=0)

    def sum_copy(r):
        return pltpu.make_async_remote_copy(
            tile_ref, box.at[r - 1], sum_send.at[r - 1], sum_recv.at[r - 1],
            device_id=(tm, (me + r) % n), device_id_type=MESH,
        )

    for r in range(1, n):
        sum_copy(r).start()
    for s in range(chips):
        pair_copy(s).wait_send()
    for s in range(chips - 1):
        chip_copy(s).wait_send()
    for r in range(1, times):
        tm_copy(r).wait_send()
    own_copy(0).wait_send()
    for r in range(1, chips):
        own_copy(r).wait_send()
        forward(r).wait_send()
    answer = tile_ref[...]
    for r in range(1, n):
        sum_copy(r).wait_recv()
        answer = answer + box[r - 1]
    lines = jnp.sum(answer, axis=1, keepdims=True) * corr_scale
    corr_ref[...] = jnp.concatenate([lines[:combos], lines[combos:]], axis=1)
    for r in range(1, n):
        sum_copy(r).wait_send()


def shards(vectors, perambulators, shift_steps, spin_choice):
    vec = vectors[0]
    _, _, nvec, sites = vec.shape
    spin_pairs = perambulators.shape[1]
    combos = spin_choice.shape[0]
    n = lax.axis_size("space")
    times = lax.axis_size("tm")
    own, half, lanes = nvec // n, nvec // 2, 2 * nvec
    chips = n // 2
    scale = 1.0 / math.sqrt(24.0 * sites * n)
    corr_scale = 0.25 / (nvec * math.sqrt(nvec))
    mats = perambulators[0].reshape(spin_pairs, 2, half, lanes)
    mats = jnp.transpose(mats, (0, 2, 1, 3)).reshape(spin_pairs, nvec, lanes)
    tile = (half * own, lanes)
    f32, bf16 = jnp.float32, jnp.bfloat16
    dma = pltpu.SemaphoreType.DMA
    smem = pl.BlockSpec(memory_space=pltpu.SMEM)
    out, correlator = pl.pallas_call(
        functools.partial(elementals_kernel, n, times, scale, corr_scale),
        out_shape=(
            jax.ShapeDtypeStruct((own, nvec, lanes), f32),
            jax.ShapeDtypeStruct((combos, 2), f32),
        ),
        in_specs=[VM, VM, smem, smem],
        out_specs=(VM, VM),
        scratch_shapes=[
            pltpu.VMEM(tile, f32),
            pltpu.VMEM((n,) + tile, f32),
            pltpu.VMEM((times - 1,) + tile, f32),
            pltpu.VMEM((2, 4 * nvec, 6 * sites), bf16),
            pltpu.VMEM((2, half * own, 6 * sites), bf16),
            pltpu.VMEM((2, half * own, 6 * sites), bf16),
            pltpu.VMEM((chips,) + tile, f32),
            pltpu.VMEM((chips,) + tile, f32),
            pltpu.VMEM((chips,) + tile, f32),
            pltpu.VMEM((chips - 1,) + tile, f32),
            pltpu.VMEM((lanes, combos * 2 * lanes), bf16),
            pltpu.VMEM((lanes, combos * 2 * lanes), bf16),
            pltpu.VMEM((combos, 2 * nvec, own * lanes), bf16),
            pltpu.VMEM((combos, 2 * nvec, own * lanes), bf16),
            pltpu.VMEM((combos * own * half, lanes), f32),
            pltpu.VMEM((combos * own * half, lanes), f32),
            pltpu.VMEM(tile, f32),
            pltpu.VMEM((nvec, lanes), f32),
            pltpu.VMEM((combos, 3, nvec, lanes), f32),
            pltpu.VMEM((2 * combos, lanes), f32),
            pltpu.VMEM((n - 1, 2 * combos, lanes), f32),
            dma((chips,)), dma((chips,)),
            dma((chips - 1,)), dma((chips - 1,)),
            dma((chips,)), dma((chips,)),
            dma((chips - 1,)), dma((chips - 1,)),
            dma((times - 1,)), dma((times - 1,)),
            dma((n - 1,)), dma((n - 1,)),
        ],
        compiler_params=pltpu.CompilerParams(
            collective_id=0, has_side_effects=True, vmem_limit_bytes=60 * 1024 * 1024
        ),
        name="elementals",
    )(vec, mats, shift_steps, spin_choice)
    out = jnp.transpose(out.reshape(own, half, 2, lanes), (0, 2, 1, 3))
    return (out.reshape(1, own, 2, nvec * nvec), correlator[None])


def solution(mesh):
    placed = (P("tm", None, None, None, "space"), P("tm", None, None, None), P("tm"), P())
    return jax.shard_map(
        shards,
        mesh=mesh,
        in_specs=placed,
        out_specs=(P("tm", "space", None, None), P("tm", None, None)),
        check_vma=False,
    )
```

profile of v0, /device:TPU:0, one launch (start us, length us, event | category | flops | bytes accessed | tf_op | source)
XLA Modules:
  0.0 46.9 jit_solution(12404553187884903741)
XLA Ops:
  1.3 42.6 %elementals.1 = (f32[8,64,128]{2,1,0:T(8,128)}, f32[4,2]{1,0:T(4,128)}) custom-call(f32[2,3,64,256]{3,2,1,0:T(8,128)} %bitcast.13, f32[16,64,128]{2,1,0:T(8,128)} %bitcast.12, s32[1]{0:T(128)S(6)} %copy.10.shift_ref, s32[4,3]{1,0:T(4,128)} %spin_ref.1), custom_call_target="tpu_custom_call" | custom-call | tf_op jit(solution)/shard_map/elementals/pallas_call | solution.py:366
  43.9 0.0 copy-start
  43.9 0.7 %copy-done = f32[4,2]{1,0:T(4,128)S(1)} copy-done((f32[4,2]{1,0:T(4,128)S(1)}, f32[4,2]{1,0:T(4,128)}, u32[]{:S(2)}) %copy-start) | copy-done | bytes 56
  44.5 0.6 %copy.8 = f32[4,2]{0,1:T(2,128)} copy(f32[4,2]{1,0:T(4,128)S(1)} %copy-done) | data formatting | bytes 64 | tf_op jit(solution)/shard_map/elementals/pallas_call | solution.py:366
  45.2 1.7 %copy.11 = f32[1,8,2,4096]{3,2,1,0:T(2,128)} copy(f32[1,8,2,4096]{3,2,1,0:T(2,128)} %bitcast.14) | data formatting | bytes 524288
Async XLA Ops:
  43.9 0.7 %copy-start = (f32[4,2]{1,0:T(4,128)S(1)}, f32[4,2]{1,0:T(4,128)}, u32[]{:S(2)}) copy-start(f32[4,2]{1,0:T(4,128)} %get-tuple-element.5) | copy-start | bytes 100
where the time goes:
time: 47.1 us; the launch traced here: 46.9 us
  Pallas kernels  42.6 us (90%)
  local copies, waits for them, and re-layouts  2.99 us (6%)
  between operations  1.29 us (3%)
    pallas_call x1, Pallas kernels, shards(): pl.pallas_call(functools.partial(elementals_kernel, n, times, scale, corr...  42.6 us
    unnamed x3, local copies, waits for them, and re-layouts  2.35 us

commit v1 on v0

v1 whole, which is shorter than its diff:
```python
import functools
import math

import jax
import jax.numpy as jnp
from jax import lax
from jax.experimental import pallas as pl
from jax.experimental.pallas import tpu as pltpu
from jax.sharding import PartitionSpec as P

MESH = pl.DeviceIdType.MESH
VM = pl.BlockSpec(memory_space=pltpu.VMEM)
NT_DIMS = (((1,), (1,)), ((), ()))


def halves(x):
    top = x.astype(jnp.bfloat16)
    return top, (x - top.astype(jnp.float32)).astype(jnp.bfloat16)


def dot(a, b):
    return jnp.dot(a, b, preferred_element_type=jnp.float32)


def elementals_kernel(
    n, times, scale, corr_scale, v_ref, mats_ref, shift_ref, spin_ref, out_ref, corr_ref,
    vv, lead, d_hi, d_lo, keep, give, pair_in, chip_in, own_ref, full, sink_ref,
    board, spin_mats, local_mats, right_hh, right_lo, left_hl, placed, dense_hl,
    half_hi, half_lo, cross_w, same_w, lc_hi, lc_lo, mid_ref, slabs, sl_hi, sl_lo,
    turn, pick, tile_ref, box,
    pair_send, pair_recv, chip_send, chip_recv,
    own_send, own_recv, fwd_send, fwd_recv, tm_send, tm_recv,
    sum_send, sum_recv,
):
    f32 = jnp.float32
    me = lax.axis_index("space")
    tm = lax.axis_index("tm")
    chips = n // 2
    chip = me // 2
    core = me % 2
    mate = chip * 2 + 1 - core
    nvec = v_ref.shape[2]
    sites = v_ref.shape[3]
    own = nvec // n
    half = nvec // 2
    lanes = 2 * nvec
    reach = half // 2
    share = own * reach
    per_half = n // 2
    wide = half + reach
    block_rows = wide * reach
    side = me // per_half
    other_side = 1 - side
    first = (me % per_half) * own
    combos = spin_ref.shape[0]
    count = combos * 3 * own
    low = -(-count // 16) * 16

    barrier = pltpu.get_barrier_semaphore()
    for r in range(1, n):
        pl.semaphore_signal(barrier, inc=1, device_id=(tm, (me + r) % n), device_id_type=MESH)
    for r in range(1, times):
        pl.semaphore_signal(
            barrier, inc=1, device_id=((tm + r) % times, me), device_id_type=MESH
        )

    for a in range(3):
        re = v_ref[0, a]
        im = v_ref[1, a]
        re_hi, re_lo = halves(re)
        im_hi, im_lo = halves(im)
        one = pl.ds(a * sites, sites)
        two = pl.ds((3 + a) * sites, sites)
        lead[0:nvec, one] = re_hi
        lead[0:nvec, two] = -im_hi
        lead[nvec:lanes, one] = im_hi
        lead[nvec:lanes, two] = re_hi
        lead[lanes:lanes + nvec, one] = re_lo
        lead[lanes:lanes + nvec, two] = -im_lo
        lead[lanes + nvec:2 * lanes, one] = im_lo
        lead[lanes + nvec:2 * lanes, two] = re_lo
        for c, value in enumerate((re, im)):
            for hf in range(2):
                part = value[hf * half:(hf + 1) * half]
                vv[c, a, hf * wide:hf * wide + half, :] = part
                vv[c, a, hf * wide + half:(hf + 1) * wide, :] = part[:reach]

    def window(c, x, start):
        return vv.at[c, x, pl.ds(start, own + reach), :]

    def fill(dest, slot):
        base = (dest // per_half) * wide + (dest % per_half) * own

        def step(a):
            if own % 8 == 0:
                start = pl.multiple_of(base, 8)
                mine = [[window(c, x, start)[a:a + 1, :] for x in range(3)] for c in range(2)]
                other = [
                    [window(c, x, start)[a + 1:a + 1 + reach, :] for x in range(3)] for c in range(2)
                ]
            else:
                mine = [[vv[c, x, pl.ds(base + a, 1), :] for x in range(3)] for c in range(2)]
                other = [
                    [
                        jnp.concatenate(
                            [vv[c, x, pl.ds(base + a + 1 + r, 1), :] for r in range(reach)], axis=0
                        )
                        for x in range(3)
                    ]
                    for c in range(2)
                ]
            at = pl.ds(pl.multiple_of(slot * share + a * reach, reach), reach)
            for m in range(3):
                b, d = (m + 1) % 3, (m + 2) % 3
                real_part = (
                    mine[0][b] * other[0][d] - mine[1][b] * other[1][d]
                    - (mine[0][d] * other[0][b] - mine[1][d] * other[1][b])
                )
                imag_part = (
                    mine[0][b] * other[1][d] + mine[1][b] * other[0][d]
                    - (mine[0][d] * other[1][b] + mine[1][d] * other[0][b])
                )
                for q, value in ((m, real_part), (3 + m, imag_part)):
                    hi, lo = halves(value)
                    d_hi[at, q * sites:(q + 1) * sites] = hi
                    d_lo[at, q * sites:(q + 1) * sites] = lo

        for a in range(own):
            step(a)

    def pair_copy(s):
        return pltpu.make_async_remote_copy(
            give.at[s], pair_in.at[s], pair_send.at[s], pair_recv.at[s],
            device_id=(tm, mate), device_id_type=MESH,
        )

    def chip_copy(s):
        return pltpu.make_async_remote_copy(
            keep.at[s], chip_in.at[s], chip_send.at[s], chip_recv.at[s],
            device_id=(tm, (chip + 1 + s) % chips * 2 + core), device_id_type=MESH,
        )

    def blocks(s):
        target = (chip + 1 + s) % chips * 2
        fill(target + 1 - core, 0)
        fill(target + core, 1)
        both = lax.dot_general(d_hi[...], lead[...], NT_DIMS, preferred_element_type=f32)
        rest = lax.dot_general(d_lo[...], lead[0:lanes], NT_DIMS, preferred_element_type=f32)
        got = both[:, :lanes] + (both[:, lanes:] + rest)
        give[s] = got[:share]
        keep[s] = got[share:]

    def one_chip(s, carry):
        blocks(s)
        pair_copy(s).start()
        pair_copy(s - 1).wait_recv()
        keep[s - 1] = keep[s - 1] + pair_in[s - 1]
        chip_copy(s - 1).start()
        return carry

    blocks(0)
    pl.semaphore_wait(barrier, n - 1 + times - 1)
    pair_copy(0).start()
    lax.fori_loop(1, chips, one_chip, 0)

    lane = lax.broadcasted_iota(jnp.int32, (half, lanes), 1)
    spot = lane % nvec
    left = spot < half
    real = lane < nvec
    minus_plus = jnp.where(lax.broadcasted_iota(jnp.int32, (nvec, lanes), 1) < nvec, -1.0, 1.0)

    def weave(ref):
        even = ref[pl.ds(0, half, stride=2), :]
        odd = ref[pl.ds(1, half, stride=2), :]
        return (
            jnp.where(real, even, pltpu.roll(odd, nvec, 1)),
            jnp.where(real, pltpu.roll(even, nvec, 1), odd),
        )

    for s in range(combos):
        for q in range(3):
            board[...] = mats_ref[spin_ref[s, q]]
            even, odd = weave(board)
            spin_mats[s, q, pl.ds(0, half, stride=2), :] = even
            spin_mats[s, q, pl.ds(1, half, stride=2), :] = odd
            near = spin_mats[s, q, pl.ds(pl.multiple_of(side * half, half), half), :]
            far = spin_mats[s, q, pl.ds(pl.multiple_of(other_side * half, half), half), :]
            local = jnp.concatenate([near, far], axis=0)
            local_mats[s, q] = local
            at = (s * 3 + q) * lanes
            top_hi, top_lo = halves(local)
            low_hi, low_lo = halves(minus_plus * pltpu.roll(local, nvec, 1))
            right_hh[0:nvec, at:at + lanes] = top_hi
            right_hh[nvec:lanes, at:at + lanes] = low_hi
            right_hh[lanes:lanes + nvec, at:at + lanes] = top_hi
            right_hh[lanes + nvec:2 * lanes, at:at + lanes] = low_hi
            right_lo[0:nvec, at:at + lanes] = top_lo
            right_lo[nvec:lanes, at:at + lanes] = low_lo
    pairs = ((1, 2), (0, 2), (0, 1))
    for s in range(combos):
        for p in range(3):
            q, r = pairs[p]
            both = jnp.transpose(jnp.concatenate([local_mats[s, q], local_mats[s, r]], axis=0))
            hi, lo = halves(both)
            left_hl[s * 3 + p, :, 0:lanes] = hi
            left_hl[s * 3 + p, :, lanes:2 * lanes] = lo
    for s in range(combos):
        for p in range(3):
            if own % 8 == 0:
                rows = spin_mats[s, p, pl.ds(pl.multiple_of(me * own, own), own), :]
                mid_ref[(s * 3 + p) * own:(s * 3 + p + 1) * own, :] = rows
            else:
                for r in range(own):
                    at = (s * 3 + p) * own + r
                    mid_ref[at:at + 1, :] = spin_mats[s, p, pl.ds(me * own + r, 1), :]

    last = chips - 1
    pair_copy(last).wait_recv()
    total = keep[last] + pair_in[last]
    for s in range(last):
        chip_copy(s).wait_recv()
        total = total + chip_in[s]
    own_ref[...] = total * scale

    def rows_of(d):
        start = (d // per_half) * block_rows + reach * reach + (d % per_half) * share
        return pl.ds(pl.multiple_of(start, reach), share)

    def tm_copy(r):
        return pltpu.make_async_remote_copy(
            own_ref, sink_ref.at[r - 1], tm_send.at[r - 1], tm_recv.at[r - 1],
            device_id=((tm + r) % times, me), device_id_type=MESH,
        )

    def own_copy(r):
        target = mate if r == 0 else (chip + r) % chips * 2 + core
        return pltpu.make_async_remote_copy(
            own_ref, full.at[rows_of(me)], own_send.at[r], own_recv.at[r],
            device_id=(tm, target), device_id_type=MESH,
        )

    def forward(r):
        at = rows_of((chip + chips - r) % chips * 2 + core)
        return pltpu.make_async_remote_copy(
            full.at[at], full.at[at], fwd_send.at[r - 1], fwd_recv.at[r - 1],
            device_id=(tm, mate), device_id_type=MESH,
        )

    for r in range(1, times):
        tm_copy(r).start()
    for r in range(1, chips):
        own_copy(r).start()
    own_copy(0).start()
    full[rows_of(me), :] = own_ref[...]

    for r in range(1, times):
        tm_copy(r).wait_recv()
    chosen = sink_ref[jnp.clip(times - 1 - shift_ref[0], 0, times - 2)]
    wide_lane = lax.broadcasted_iota(jnp.int32, (share, lanes), 1)
    wide_left = wide_lane % nvec < half
    swapped = jnp.where(wide_left, pltpu.roll(chosen, lanes - half, 1), pltpu.roll(chosen, half, 1))
    chosen = jnp.where(side == 1, swapped, chosen)
    step_of = lax.broadcasted_iota(jnp.int32, (share, lanes), 0) % reach
    factor = jnp.where(wide_left, 1.0 / 3.0, 1.0) * jnp.where(step_of == reach - 1, 0.5, 1.0)
    chosen = chosen * jnp.where(wide_lane < nvec, factor, -factor)
    placed[...] = jnp.zeros_like(placed)
    for a in range(own):
        if own % 8 == 0:
            start = pl.multiple_of(a * wide + first, 8)
            view = placed.at[pl.ds(start, own + reach), :]
            view[a + 1:a + 1 + reach, :] = chosen[a * reach:(a + 1) * reach]
        else:
            for r in range(reach):
                at = a * wide + first + a + 1 + r
                placed[pl.ds(at, 1), :] = chosen[a * reach + r:a * reach + r + 1]
    around = [
        placed[a * wide:a * wide + half, :] + jnp.concatenate(
            [placed[a * wide + half:(a + 1) * wide, :], jnp.zeros((half - reach, lanes), f32)], axis=0
        )
        for a in range(own)
    ]
    fold = lanes // half
    for g in range(0, own, fold):
        group = (around[g:g + fold] * fold)[:fold]
        t = jnp.transpose(jnp.concatenate(group, axis=0))
        for a in range(g, min(g + fold, own)):
            at = (a % fold) * half
            back = (lanes - at) % lanes

            def to_left(re, im):
                re = pltpu.roll(re, back, 1) if back else re
                im = pltpu.roll(im, (back + nvec) % lanes, 1) if (back + nvec) % lanes else im
                return jnp.where(left, jnp.where(real, re, im), 0.0)

            top = around[a] - to_left(t[:half], t[nvec:nvec + half])
            bottom = -to_left(t[half:nvec], t[nvec + half:])
            hi, lo = halves(jnp.concatenate([top, bottom], axis=0))
            dense_hl[a * nvec:(a + 1) * nvec, 0:lanes] = hi
            dense_hl[a * nvec:(a + 1) * nvec, lanes:2 * lanes] = lo

    for s in range(combos):
        at = s * 3 * lanes
        got = dot(dense_hl[...], right_hh[:, at:at + 3 * lanes]) + dot(
            dense_hl[:, 0:lanes], right_lo[:, at:at + 3 * lanes]
        )
        hi, lo = halves(got)
        for q in range(3):
            for a in range(own):
                where = (s * 3 + q, slice(None), pl.ds(a * lanes, lanes))
                half_hi[where] = hi[a * nvec:(a + 1) * nvec, q * lanes:(q + 1) * lanes]
                half_lo[where] = lo[a * nvec:(a + 1) * nvec, q * lanes:(q + 1) * lanes]
    for s in range(combos):
        for p in range(3):
            q, r = pairs[p]
            m = s * 3 + p
            r_hi = jnp.concatenate([half_hi[s * 3 + r], half_hi[s * 3 + q]], axis=0)
            r_lo = jnp.concatenate([half_lo[s * 3 + r], half_lo[s * 3 + q]], axis=0)
            got = dot(left_hl[m], jnp.concatenate([r_hi, r_hi], axis=0)) + dot(
                left_hl[m, :, 0:lanes], r_lo
            )
            for a in range(own):
                at = a * lanes
                whole = got[:nvec, at:at + lanes] + minus_plus * pltpu.roll(
                    got[nvec:, at:at + lanes], nvec, 1
                )
                rows = pl.ds((m * own + a) * half, half)
                cross_w[rows, :] = jnp.where(left, whole[half:], whole[:half])
                same_w[rows, :] = -0.5 * jnp.where(left, whole[:half], whole[half:])
    c_real = lax.broadcasted_iota(jnp.int32, (count, lanes), 1) < nvec
    for m in range(half // 2):
        even = same_w[pl.ds(2 * m, count, stride=half), :]
        odd = same_w[pl.ds(2 * m + 1, count, stride=half), :]
        re = jnp.where(c_real, even, pltpu.roll(odd, nvec, 1))
        im = jnp.where(c_real, pltpu.roll(even, nvec, 1), odd)
        at = pl.ds(m * lanes, lanes)
        for start, value in ((0, re), (low, im)):
            hi, lo = halves(value)
            lc_hi[start:start + count, at] = hi
            lc_lo[start:start + count, at] = lo

    for r in range(1, chips):
        own_copy(r).wait_recv()
        forward(r).start()
    own_copy(0).wait_recv()
    for r in range(1, chips):
        forward(r).wait_recv()
    for hf in range(2):
        at = hf * block_rows
        full[at:at + reach * reach, :] = full[at + half * reach:at + block_rows, :]

    inner = lax.broadcasted_iota(jnp.int32, (reach, lanes), 0)
    spot64 = lax.broadcasted_iota(jnp.int32, (nvec, lanes), 1) % nvec
    row64 = lax.broadcasted_iota(jnp.int32, (nvec, lanes), 0)
    crossing = (spot64 >= half) == (row64 < half)
    c_sign = jnp.where(c_real, -1.0, 1.0)
    mid = mid_ref[...]
    turned = pltpu.roll(mid, nvec, 1)
    pad = [jnp.zeros((low - count, nvec), jnp.bfloat16)] if low > count else []
    re_hi, re_lo = halves(mid[:, :nvec])
    im_hi, im_lo = halves(turned[:, :nvec])
    mid_hi = jnp.concatenate([re_hi] + pad + [im_hi], axis=0)
    mid_lo = jnp.concatenate([re_lo] + pad + [im_lo], axis=0)
    mid_k = jnp.concatenate([mid_hi, mid_hi, mid_lo], axis=1)
    one = jnp.zeros((count, lanes), f32)
    two = jnp.zeros((count, lanes), f32)
    for y in range(0, half, 2):
        pair = []
        for k in (y, y + 1):
            parts = []
            for hf in range(2):
                at = hf * block_rows
                before = full[pl.ds(at + reach * k + reach - 1, reach, stride=reach - 1), :]
                behind = full[pl.ds(at + reach * reach + reach * k - 1, reach), :]
                behind = jnp.where(inner == 0, 0.0, -behind)
                slab = jnp.concatenate([before, behind], axis=0)
                shift = (k - reach) % half
                if shift:
                    slab = pltpu.roll(slab, shift, 0)
                slabs[hf * half + k] = slab
                parts.append(slab)
            slab = jnp.concatenate(parts, axis=0)
            hi, lo = halves(slab)
            sl_hi[k * nvec:(k + 1) * nvec, :] = hi
            sl_lo[k * nvec:(k + 1) * nvec, :] = lo
            m_hi, m_lo = halves(jnp.where(crossing, slab, 0.0))
            pair.append(jnp.concatenate([m_hi, m_lo, m_hi], axis=0))
        got = dot(mid_k, jnp.concatenate(pair, axis=1))
        for b, k in enumerate((y, y + 1)):
            here = got[:, b * lanes:(b + 1) * lanes]
            value = here[:count] + c_sign * pltpu.roll(here[low:low + count], nvec, 1)
            weight = cross_w[pl.ds(k, count, stride=half), :]
            one = one + value * weight
            two = two + value * pltpu.roll(weight, nvec, 1)
    got = dot(lc_hi[...], sl_hi[...]) + (dot(lc_hi[...], sl_lo[...]) + dot(lc_lo[...], sl_hi[...]))
    value = got[:count] + c_sign * pltpu.roll(got[low:low + count], nvec, 1)
    one = one + value * mid
    two = two + value * turned
    one = jnp.where(c_real, one, -one)
    each = 3 * own
    tile_ref[...] = jnp.concatenate(
        [jnp.sum(one[s * each:(s + 1) * each], axis=0, keepdims=True) for s in range(combos)]
        + [jnp.sum(two[s * each:(s + 1) * each], axis=0, keepdims=True) for s in range(combos)],
        axis=0,
    )

    def sum_copy(r):
        return pltpu.make_async_remote_copy(
            tile_ref, box.at[r - 1], sum_send.at[r - 1], sum_recv.at[r - 1],
            device_id=(tm, (me + r) % n), device_id_type=MESH,
        )

    for r in range(1, n):
        sum_copy(r).start()

    for g in range(half // fold):
        t = jnp.transpose(jnp.concatenate(
            [slabs[other_side * half + g * fold + q] for q in range(fold)], axis=0
        ))
        turn[...] = t
        if own % 8 == 0:
            at = pl.multiple_of(side * half + first, own)
            pick[0, g * own:(g + 1) * own, :] = turn[pl.ds(at, own), :]
            pick[1, g * own:(g + 1) * own, :] = turn[pl.ds(at + nvec, own), :]
        else:
            for r in range(own):
                at = side * half + first + r
                pick[0, g * own + r:g * own + r + 1, :] = turn[pl.ds(at, 1), :]
                pick[1, g * own + r:g * own + r + 1, :] = turn[pl.ds(at + nvec, 1), :]
    steps = half // fold
    quarter = lax.broadcasted_iota(jnp.int32, (steps, lanes), 1) // half
    o_left = lax.broadcasted_iota(jnp.int32, (steps, lanes), 1) % nvec < half

    def shifted(x, by):
        by = by % lanes
        return pltpu.roll(x, by, 1) if by else x

    for g in range(0, own, fold):
        group = [slabs[side * half + first + a] for a in range(g, min(g + fold, own))]
        turn[...] = jnp.transpose(jnp.concatenate((group * fold)[:fold], axis=0))
        at = pl.multiple_of(other_side * half, half)
        re = turn[pl.ds(at, half), :]
        im = turn[pl.ds(at + nvec, half), :]
        turn[0:half, :] = re
        turn[half:2 * half, :] = im
        for a in range(g, min(g + fold, own)):
            for q in range(fold):
                x_re = turn[pl.ds(q, steps, stride=fold), :]
                x_im = turn[pl.ds(half + q, steps, stride=fold), :]
                c_re = pick[0, pl.ds(a, steps, stride=own), :]
                c_im = pick[1, pl.ds(a, steps, stride=own), :]
                back = (a % fold) * half
                value = jnp.where(
                    quarter < 2,
                    jnp.where(quarter == 0, -shifted(x_re, -back), shifted(c_re, half - q * half)),
                    jnp.where(quarter == 2, -shifted(x_im, nvec - back), shifted(c_im, nvec + half - q * half)),
                )
                flipped = jnp.where(o_left, pltpu.roll(value, lanes - half, 1), pltpu.roll(value, half, 1))
                value = jnp.where(side == 1, flipped, value)
                placed[pl.ds(q, steps, stride=fold), :] = value
            board[pl.ds(pl.multiple_of(side * half, half), half), :] = slabs[side * half + first + a]
            board[pl.ds(pl.multiple_of(other_side * half, half), half), :] = placed[0:half, :]
            even, odd = weave(board)
            out_ref[a, pl.ds(0, half, stride=2), :] = even
            out_ref[a, pl.ds(1, half, stride=2), :] = odd

    for s in range(chips):
        pair_copy(s).wait_send()
    for s in range(chips - 1):
        chip_copy(s).wait_send()
    for r in range(1, times):
        tm_copy(r).wait_send()
    own_copy(0).wait_send()
    for r in range(1, chips):
        own_copy(r).wait_send()
        forward(r).wait_send()
    answer = tile_ref[...]
    for r in range(1, n):
        sum_copy(r).wait_recv()
        answer = answer + box[r - 1]
    lines = jnp.sum(answer, axis=1, keepdims=True) * corr_scale
    corr_ref[...] = jnp.concatenate([lines[:combos], lines[combos:]], axis=1)
    for r in range(1, n):
        sum_copy(r).wait_send()


def shards(vectors, perambulators, shift_steps, spin_choice):
    vec = vectors[0]
    _, _, nvec, sites = vec.shape
    spin_pairs = perambulators.shape[1]
    combos = spin_choice.shape[0]
    n = lax.axis_size("space")
    times = lax.axis_size("tm")
    own, half, lanes = nvec // n, nvec // 2, 2 * nvec
    reach = half // 2
    wide = half + reach
    share = own * reach
    chips = n // 2
    count = combos * 3 * own
    low = -(-count // 16) * 16
    scale = 1.0 / math.sqrt(24.0 * sites * n)
    corr_scale = 0.25 / (nvec * math.sqrt(nvec))
    mats = perambulators[0].reshape(spin_pairs, 2, half, lanes)
    mats = jnp.transpose(mats, (0, 2, 1, 3)).reshape(spin_pairs, nvec, lanes)
    tile = (share, lanes)
    f32, bf16 = jnp.float32, jnp.bfloat16
    dma = pltpu.SemaphoreType.DMA
    smem = pl.BlockSpec(memory_space=pltpu.SMEM)
    out, correlator = pl.pallas_call(
        functools.partial(elementals_kernel, n, times, scale, corr_scale),
        out_shape=(
            jax.ShapeDtypeStruct((own, nvec, lanes), f32),
            jax.ShapeDtypeStruct((combos, 2), f32),
        ),
        in_specs=[VM, VM, smem, smem],
        out_specs=(VM, VM),
        scratch_shapes=[
            pltpu.VMEM((2, 3, 2 * wide, sites), f32),
            pltpu.VMEM((4 * nvec, 6 * sites), bf16),
            pltpu.VMEM((2 * share, 6 * sites), bf16),
            pltpu.VMEM((2 * share, 6 * sites), bf16),
            pltpu.VMEM((chips,) + tile, f32),
            pltpu.VMEM((chips,) + tile, f32),
            pltpu.VMEM((chips,) + tile, f32),
            pltpu.VMEM((chips - 1,) + tile, f32),
            pltpu.VMEM(tile, f32),
            pltpu.VMEM((2 * wide * reach, lanes), f32),
            pltpu.VMEM((times - 1,) + tile, f32),
            pltpu.VMEM((nvec, lanes), f32),
            pltpu.VMEM((combos, 3, nvec, lanes), f32),
            pltpu.VMEM((combos, 3, nvec, lanes), f32),
            pltpu.VMEM((2 * lanes, combos * 3 * lanes), bf16),
            pltpu.VMEM((lanes, combos * 3 * lanes), bf16),
            pltpu.VMEM((combos * 3, lanes, 2 * lanes), bf16),
            pltpu.VMEM((max(own, 2) * wide, lanes), f32),
            pltpu.VMEM((own * nvec, 2 * lanes), bf16),
            pltpu.VMEM((combos * 3, nvec, own * lanes), bf16),
            pltpu.VMEM((combos * 3, nvec, own * lanes), bf16),
            pltpu.VMEM((count * half, lanes), f32),
            pltpu.VMEM((count * half, lanes), f32),
            pltpu.VMEM((2 * low, half * nvec), bf16),
            pltpu.VMEM((2 * low, half * nvec), bf16),
            pltpu.VMEM((count, lanes), f32),
            pltpu.VMEM((nvec, half, lanes), f32),
            pltpu.VMEM((half * nvec, lanes), bf16),
            pltpu.VMEM((half * nvec, lanes), bf16),
            pltpu.VMEM((lanes, lanes), f32),
            pltpu.VMEM((2, own * (nvec // 8), lanes), f32),
            pltpu.VMEM((2 * combos, lanes), f32),
            pltpu.VMEM((n - 1, 2 * combos, lanes), f32),
            dma((chips,)), dma((chips,)),
            dma((chips - 1,)), dma((chips - 1,)),
            dma((chips,)), dma((chips,)),
            dma((chips - 1,)), dma((chips - 1,)),
            dma((times - 1,)), dma((times - 1,)),
            dma((n - 1,)), dma((n - 1,)),
        ],
        compiler_params=pltpu.CompilerParams(
            collective_id=0, has_side_effects=True, vmem_limit_bytes=60 * 1024 * 1024
        ),
        name="elementals",
    )(vec, mats, shift_steps, spin_choice)
    out = jnp.transpose(out.reshape(own, half, 2, lanes), (0, 2, 1, 3))
    return (out.reshape(1, own, 2, nvec * nvec), correlator[None])


def solution(mesh):
    placed = (P("tm", None, None, None, "space"), P("tm", None, None, None), P("tm"), P())
    return jax.shard_map(
        shards,
        mesh=mesh,
        in_specs=placed,
        out_specs=(P("tm", "space", None, None), P("tm", None, None)),
        check_vma=False,
    )
```

time: 47.1 us -> 37 us (0.79)
  Pallas kernels: 42.6 us -> 32.6 us
    pallas_call x1, Pallas kernels: 42.6 us -> 32.6 us  [shards(): pl.pallas_call(functools.partial(elementals_kernel, n, times, scale, corr...]
where the time goes in v1:
time: 37 us; the launch traced here: 36.8 us
  Pallas kernels  32.6 us (88%)
  local copies, waits for them, and re-layouts  2.99 us (8%)
  between operations  1.29 us (3%)
    pallas_call x1, Pallas kernels, shards(): pl.pallas_call(functools.partial(elementals_kernel, n, times, scale, corr...  32.6 us
    unnamed x3, local copies, waits for them, and re-layouts  2.35 us

profile of v1, /device:TPU:0, one launch (start us, length us, event | category | flops | bytes accessed | tf_op | source)
XLA Modules:
  0.0 36.8 jit_solution(16545299093598696313)
XLA Ops:
  1.3 32.6 %elementals.1 = (f32[8,64,128]{2,1,0:T(8,128)}, f32[4,2]{1,0:T(4,128)}) custom-call(f32[2,3,64,256]{3,2,1,0:T(8,128)} %bitcast.13, f32[16,64,128]{2,1,0:T(8,128)} %bitcast.12, s32[1]{0:T(128)S(6)} %copy.10.shift_ref, s32[4,3]{1,0:T(4,128)} %spin_ref.1), custom_call_target="tpu_custom_call" | custom-call | tf_op jit(solution)/shard_map/elementals/pallas_call | solution.py:508
  33.8 0.0 copy-start
  33.8 0.7 %copy-done = f32[4,2]{1,0:T(4,128)S(1)} copy-done((f32[4,2]{1,0:T(4,128)S(1)}, f32[4,2]{1,0:T(4,128)}, u32[]{:S(2)}) %copy-start) | copy-done | bytes 56
  34.5 0.6 %copy.8 = f32[4,2]{0,1:T(2,128)} copy(f32[4,2]{1,0:T(4,128)S(1)} %copy-done) | data formatting | bytes 64 | tf_op jit(solution)/shard_map/elementals/pallas_call | solution.py:508
  35.2 1.7 %copy.11 = f32[1,8,2,4096]{3,2,1,0:T(2,128)} copy(f32[1,8,2,4096]{3,2,1,0:T(2,128)} %bitcast.14) | data formatting | bytes 524288
Async XLA Ops:
  33.8 0.7 %copy-start = (f32[4,2]{1,0:T(4,128)S(1)}, f32[4,2]{1,0:T(4,128)}, u32[]{:S(2)}) copy-start(f32[4,2]{1,0:T(4,128)} %get-tuple-element.5) | copy-start | bytes 100

commit v2 on v1

--- a/solution.py
+++ b/solution.py
@@ -23,8 +23,8 @@
 
 
 def elementals_kernel(
-    n, times, scale, corr_scale, v_ref, mats_ref, shift_ref, spin_ref, out_ref, corr_ref,
-    vv, lead, d_hi, d_lo, keep, give, pair_in, chip_in, own_ref, full, sink_ref,
+    n, times, scale, corr_scale, v_hbm, mats_hbm, shift_hbm, spin_ref, out_ref, corr_ref,
+    v_ref, mats_ref, shift_ref, in_sem, vv, lead, d_hi, d_lo, keep, give, pair_in, chip_in, own_ref, full, sink_ref,
     board, spin_mats, local_mats, right_hh, right_lo, left_hl, placed, dense_hl,
     half_hi, half_lo, cross_w, same_w, lc_hi, lc_lo, mid_ref, slabs, sl_hi, sl_lo,
     turn, pick, tile_ref, box,
@@ -56,6 +56,16 @@
     count = combos * 3 * own
     low = -(-count // 16) * 16
 
+    def partner(m, back=False):
+        if chips & (chips - 1):
+            return (chip + chips - m) % chips if back else (chip + m) % chips
+        out, bit = 0, 1
+        while bit < chips:
+            mine, its = chip // bit % 2, m // bit % 2
+            out = out + bit * (mine + its - 2 * mine * its)
+            bit *= 2
+        return out
+
     barrier = pltpu.get_barrier_semaphore()
     for r in range(1, n):
         pl.semaphore_signal(barrier, inc=1, device_id=(tm, (me + r) % n), device_id_type=MESH)
@@ -63,6 +73,14 @@
         pl.semaphore_signal(
             barrier, inc=1, device_id=((tm + r) % times, me), device_id_type=MESH
         )
+
+    loads = [
+        pltpu.make_async_copy(src, dst, in_sem.at[i])
+        for i, (src, dst) in enumerate(((v_hbm, v_ref), (mats_hbm, mats_ref), (shift_hbm, shift_ref)))
+    ]
+    for load in loads:
+        load.start()
+    loads[0].wait()
 
     for a in range(3):
         re = v_ref[0, a]
@@ -82,51 +100,36 @@
         for c, value in enumerate((re, im)):
             for hf in range(2):
                 part = value[hf * half:(hf + 1) * half]
-                vv[c, a, hf * wide:hf * wide + half, :] = part
-                vv[c, a, hf * wide + half:(hf + 1) * wide, :] = part[:reach]
-
-    def window(c, x, start):
-        return vv.at[c, x, pl.ds(start, own + reach), :]
-
-    def fill(dest, slot):
+                for b in range(sites // 128):
+                    cut = part[:, b * 128:(b + 1) * 128]
+                    vv[c, a, b, pl.ds(2 * hf * wide, half, stride=2), :] = cut
+                    vv[c, a, b, pl.ds(2 * (hf * wide + half), reach, stride=2), :] = cut[:reach]
+
+    def fill(dest, slot, buf):
         base = (dest // per_half) * wide + (dest % per_half) * own
-
-        def step(a):
-            if own % 8 == 0:
-                start = pl.multiple_of(base, 8)
-                mine = [[window(c, x, start)[a:a + 1, :] for x in range(3)] for c in range(2)]
+        for a in range(own):
+            at = pl.ds(slot * share + a * reach, reach)
+            for cut in range(sites // 128):
+                mine = [[vv[c, x, cut, pl.ds(2 * (base + a), 1), :] for x in range(3)] for c in range(2)]
                 other = [
-                    [window(c, x, start)[a + 1:a + 1 + reach, :] for x in range(3)] for c in range(2)
-                ]
-            else:
-                mine = [[vv[c, x, pl.ds(base + a, 1), :] for x in range(3)] for c in range(2)]
-                other = [
-                    [
-                        jnp.concatenate(
-                            [vv[c, x, pl.ds(base + a + 1 + r, 1), :] for r in range(reach)], axis=0
-                        )
-                        for x in range(3)
-                    ]
+                    [vv[c, x, cut, pl.ds(2 * (base + a + 1), reach, stride=2), :] for x in range(3)]
                     for c in range(2)
                 ]
-            at = pl.ds(pl.multiple_of(slot * share + a * reach, reach), reach)
-            for m in range(3):
-                b, d = (m + 1) % 3, (m + 2) % 3
-                real_part = (
-                    mine[0][b] * other[0][d] - mine[1][b] * other[1][d]
-                    - (mine[0][d] * other[0][b] - mine[1][d] * other[1][b])
-                )
-                imag_part = (
-                    mine[0][b] * other[1][d] + mine[1][b] * other[0][d]
-                    - (mine[0][d] * other[1][b] + mine[1][d] * other[0][b])
-                )
-                for q, value in ((m, real_part), (3 + m, imag_part)):
-                    hi, lo = halves(value)
-                    d_hi[at, q * sites:(q + 1) * sites] = hi
-                    d_lo[at, q * sites:(q + 1) * sites] = lo
-
-        for a in range(own):
-            step(a)
+                for m in range(3):
+                    b, d = (m + 1) % 3, (m + 2) % 3
+                    real_part = (
+                        mine[0][b] * other[0][d] - mine[1][b] * other[1][d]
+                        - (mine[0][d] * other[0][b] - mine[1][d] * other[1][b])
+                    )
+                    imag_part = (
+                        mine[0][b] * other[1][d] + mine[1][b] * other[0][d]
+                        - (mine[0][d] * other[1][b] + mine[1][d] * other[0][b])
+                    )
+                    for q, value in ((m, real_part), (3 + m, imag_part)):
+                        hi, lo = halves(value)
+                        where = q * sites + cut * 128
+                        d_hi[buf, at, where:where + 128] = hi
+                        d_lo[buf, at, where:where + 128] = lo
 
     def pair_copy(s):
         return pltpu.make_async_remote_copy(
@@ -137,31 +140,49 @@
     def chip_copy(s):
         return pltpu.make_async_remote_copy(
             keep.at[s], chip_in.at[s], chip_send.at[s], chip_recv.at[s],
-            device_id=(tm, (chip + 1 + s) % chips * 2 + core), device_id_type=MESH,
-        )
-
-    def blocks(s):
-        target = (chip + 1 + s) % chips * 2
-        fill(target + 1 - core, 0)
-        fill(target + core, 1)
-        both = lax.dot_general(d_hi[...], lead[...], NT_DIMS, preferred_element_type=f32)
-        rest = lax.dot_general(d_lo[...], lead[0:lanes], NT_DIMS, preferred_element_type=f32)
+            device_id=(tm, partner(chips - 1 - s) * 2 + core), device_id_type=MESH,
+        )
+
+    def fills(s, buf):
+        target = partner(chips - 1 - s) * 2
+        fill(target + 1 - core, 0, buf)
+        fill(target + core, 1, buf)
+
+    def products(s, buf):
+        both = lax.dot_general(d_hi[buf], lead[...], NT_DIMS, preferred_element_type=f32)
+        rest = lax.dot_general(d_lo[buf], lead[0:lanes], NT_DIMS, preferred_element_type=f32)
         got = both[:, :lanes] + (both[:, lanes:] + rest)
         give[s] = got[:share]
         keep[s] = got[share:]
 
+    def relay(s):
+        pair_copy(s).wait_recv()
+        keep[s] = keep[s] + pair_in[s]
+        chip_copy(s).start()
+
     def one_chip(s, carry):
-        blocks(s)
+        fills(s, 0)
+        products(s, 0)
         pair_copy(s).start()
-        pair_copy(s - 1).wait_recv()
-        keep[s - 1] = keep[s - 1] + pair_in[s - 1]
-        chip_copy(s - 1).start()
+        relay(s - 1)
         return carry
 
-    blocks(0)
-    pl.semaphore_wait(barrier, n - 1 + times - 1)
-    pair_copy(0).start()
-    lax.fori_loop(1, chips, one_chip, 0)
+    fills(0, 0)
+    if chips <= 4:
+        for s in range(chips):
+            products(s, s % 2)
+            if s < chips - 1:
+                fills(s + 1, (s + 1) % 2)
+            if s == 0:
+                pl.semaphore_wait(barrier, n - 1 + times - 1)
+            pair_copy(s).start()
+            if s:
+                relay(s - 1)
+    else:
+        products(0, 0)
+        pl.semaphore_wait(barrier, n - 1 + times - 1)
+        pair_copy(0).start()
+        lax.fori_loop(1, chips, one_chip, 0)
 
     lane = lax.broadcasted_iota(jnp.int32, (half, lanes), 1)
     spot = lane % nvec
@@ -177,6 +198,8 @@
             jnp.where(real, pltpu.roll(even, nvec, 1), odd),
         )
 
+    loads[1].wait()
+    loads[2].wait()
     for s in range(combos):
         for q in range(3):
             board[...] = mats_ref[spin_ref[s, q]]
@@ -233,14 +256,14 @@
         )
 
     def own_copy(r):
-        target = mate if r == 0 else (chip + r) % chips * 2 + core
+        target = mate if r == 0 else partner(r) * 2 + core
         return pltpu.make_async_remote_copy(
             own_ref, full.at[rows_of(me)], own_send.at[r], own_recv.at[r],
             device_id=(tm, target), device_id_type=MESH,
         )
 
     def forward(r):
-        at = rows_of((chip + chips - r) % chips * 2 + core)
+        at = rows_of(partner(r, True) * 2 + core)
         return pltpu.make_async_remote_copy(
             full.at[at], full.at[at], fwd_send.at[r - 1], fwd_recv.at[r - 1],
             device_id=(tm, mate), device_id_type=MESH,
@@ -248,7 +271,7 @@
 
     for r in range(1, times):
         tm_copy(r).start()
-    for r in range(1, chips):
+    for r in range(chips - 1, 0, -1):
         own_copy(r).start()
     own_copy(0).start()
     full[rows_of(me), :] = own_ref[...]
@@ -326,6 +349,9 @@
                 rows = pl.ds((m * own + a) * half, half)
                 cross_w[rows, :] = jnp.where(left, whole[half:], whole[:half])
                 same_w[rows, :] = -0.5 * jnp.where(left, whole[:half], whole[half:])
+    for r in range(1, chips):
+        own_copy(r).wait_recv()
+        forward(r).start()
     c_real = lax.broadcasted_iota(jnp.int32, (count, lanes), 1) < nvec
     for m in range(half // 2):
         even = same_w[pl.ds(2 * m, count, stride=half), :]
@@ -338,9 +364,6 @@
             lc_hi[start:start + count, at] = hi
             lc_lo[start:start + count, at] = lo
 
-    for r in range(1, chips):
-        own_copy(r).wait_recv()
-        forward(r).start()
     own_copy(0).wait_recv()
     for r in range(1, chips):
         forward(r).wait_recv()
@@ -477,8 +500,8 @@
     for r in range(1, n):
         sum_copy(r).wait_recv()
         answer = answer + box[r - 1]
-    lines = jnp.sum(answer, axis=1, keepdims=True) * corr_scale
-    corr_ref[...] = jnp.concatenate([lines[:combos], lines[combos:]], axis=1)
+    total = jnp.sum(jnp.transpose(answer), axis=0, keepdims=True) * corr_scale
+    corr_ref[...] = jnp.concatenate([total[:, :combos], total[:, combos:]], axis=0)
     for r in range(1, n):
         sum_copy(r).wait_send()
 
@@ -505,19 +528,24 @@
     f32, bf16 = jnp.float32, jnp.bfloat16
     dma = pltpu.SemaphoreType.DMA
     smem = pl.BlockSpec(memory_space=pltpu.SMEM)
+    anywhere = pl.BlockSpec(memory_space=pl.ANY)
     out, correlator = pl.pallas_call(
         functools.partial(elementals_kernel, n, times, scale, corr_scale),
         out_shape=(
-            jax.ShapeDtypeStruct((own, nvec, lanes), f32),
-            jax.ShapeDtypeStruct((combos, 2), f32),
+            pltpu.VMEM((own, nvec, lanes), f32),
+            pltpu.VMEM((2, combos), f32),
         ),
-        in_specs=[VM, VM, smem, smem],
+        in_specs=[anywhere, anywhere, anywhere, smem],
         out_specs=(VM, VM),
         scratch_shapes=[
-            pltpu.VMEM((2, 3, 2 * wide, sites), f32),
+            pltpu.VMEM(vec.shape, f32),
+            pltpu.VMEM(mats.shape, f32),
+            pltpu.SMEM(shift_steps.shape, jnp.int32),
+            dma((3,)),
+            pltpu.VMEM((2, 3, sites // 128, 4 * wide, 128), f32),
             pltpu.VMEM((4 * nvec, 6 * sites), bf16),
-            pltpu.VMEM((2 * share, 6 * sites), bf16),
-            pltpu.VMEM((2 * share, 6 * sites), bf16),
+            pltpu.VMEM((2, 2 * share, 6 * sites), bf16),
+            pltpu.VMEM((2, 2 * share, 6 * sites), bf16),
             pltpu.VMEM((chips,) + tile, f32),
             pltpu.VMEM((chips,) + tile, f32),
             pltpu.VMEM((chips,) + tile, f32),
@@ -560,7 +588,7 @@
         name="elementals",
     )(vec, mats, shift_steps, spin_choice)
     out = jnp.transpose(out.reshape(own, half, 2, lanes), (0, 2, 1, 3))
-    return (out.reshape(1, own, 2, nvec * nvec), correlator[None])
+    return (out.reshape(1, own, 2, nvec * nvec), jnp.transpose(correlator)[None])
 
 
 def solution(mesh):

time: 37 us -> 34.6 us (0.935)
  local copies, waits for them, and re-layouts: 2.99 us -> 1.27 us
  Pallas kernels: 32.6 us -> 31.9 us
    unnamed x3 -> x2, local copies, waits for them, and re-layouts: 2.35 us -> 1.27 us
    pallas_call x1 -> x0, local copies, waits for them, and re-layouts: 0.65 us -> none  [shards(): pl.pallas_call(functools.partial(elementals_kernel, n, times, scale, corr...]
    pallas_call x1, Pallas kernels: 32.6 us -> 31.9 us  [shards(): pl.pallas_call(functools.partial(elementals_kernel, n, times, scale, corr...]
where the time goes in v2:
time: 34.6 us; the launch traced here: 34.5 us
  Pallas kernels  31.9 us (92%)
  between operations  1.28 us (4%)
  local copies, waits for them, and re-layouts  1.27 us (4%)
    pallas_call x1, Pallas kernels, shards(): pl.pallas_call(functools.partial(elementals_kernel, n, times, scale, corr...  31.9 us
    unnamed x2, local copies, waits for them, and re-layouts  1.27 us

profile of v2, /device:TPU:0, one launch (start us, length us, event | category | flops | bytes accessed | tf_op | source)
XLA Modules:
  0.0 34.5 jit_solution(10904096636376982015)
XLA Ops:
  1.3 31.9 %elementals.1 = (f32[8,64,128]{2,1,0:T(8,128)S(1)}, f32[2,4]{1,0:T(2,128)S(1)}) custom-call(f32[2,3,64,256]{3,2,1,0:T(8,128)} %bitcast.17, f32[16,64,128]{2,1,0:T(8,128)} %bitcast.16, s32[1]{0:T(128)S(6)} %copy.12.shift_hbm, s32[4,3]{1,0:T(4,128)} %spin_ref.1), custom_call_target="tpu_custom_call" | custom-call | tf_op jit(solution)/shard_map/elementals/pallas_call | solution.py:532
  33.2 0.7 %copy.10 = f32[1,8,2,4096]{3,2,1,0:T(2,128)} copy(f32[1,8,2,4096]{3,2,1,0:T(2,128)S(1)} %bitcast.14) | data formatting | bytes 524288
  33.9 0.6 %copy.11 = f32[1,4,2]{1,2,0:T(2,128)} copy(f32[1,4,2]{1,2,0:T(2,128)S(1)} %bitcast.15) | data formatting | bytes 64

commit v3 on v2

--- a/solution.py
+++ b/solution.py
@@ -25,8 +25,8 @@
 def elementals_kernel(
     n, times, scale, corr_scale, v_hbm, mats_hbm, shift_hbm, spin_ref, out_ref, corr_ref,
     v_ref, mats_ref, shift_ref, in_sem, vv, lead, d_hi, d_lo, keep, give, pair_in, chip_in, own_ref, full, sink_ref,
-    board, spin_mats, local_mats, right_hh, right_lo, left_hl, placed, dense_hl,
-    half_hi, half_lo, cross_w, same_w, lc_hi, lc_lo, mid_ref, slabs, sl_hi, sl_lo,
+    board, spin_mats, local_mats, right_hl, left_hl, placed, dense_hh, dense_lo,
+    inner_ref, inner_hi, inner_lo, cross_w, same_w, lc_hi, lc_lo, mid_ref, slabs, sl_hl,
     turn, pick, tile_ref, box,
     pair_send, pair_recv, chip_send, chip_recv,
     own_send, own_recv, fwd_send, fwd_recv, tm_send, tm_recv,
@@ -74,15 +74,22 @@
             barrier, inc=1, device_id=((tm + r) % times, me), device_id_type=MESH
         )
 
-    loads = [
-        pltpu.make_async_copy(src, dst, in_sem.at[i])
-        for i, (src, dst) in enumerate(((v_hbm, v_ref), (mats_hbm, mats_ref), (shift_hbm, shift_ref)))
+    vec_loads = [
+        [
+            pltpu.make_async_copy(v_hbm.at[c, a], v_ref.at[c, a], in_sem.at[c * 3 + a])
+            for a in range(3)
+        ]
+        for c in range(2)
     ]
-    for load in loads:
-        load.start()
-    loads[0].wait()
-
+    mat_load = pltpu.make_async_copy(mats_hbm, mats_ref, in_sem.at[6])
+    shift_load = pltpu.make_async_copy(shift_hbm, shift_ref, in_sem.at[7])
     for a in range(3):
+        vec_loads[0][a].start()
+        vec_loads[1][a].start()
+
+    for a in range(3):
+        vec_loads[0][a].wait()
+        vec_loads[1][a].wait()
         re = v_ref[0, a]
         im = v_ref[1, a]
         re_hi, re_lo = halves(re)
@@ -104,6 +111,9 @@
                     cut = part[:, b * 128:(b + 1) * 128]
                     vv[c, a, b, pl.ds(2 * hf * wide, half, stride=2), :] = cut
                     vv[c, a, b, pl.ds(2 * (hf * wide + half), reach, stride=2), :] = cut[:reach]
+
+    mat_load.start()
+    shift_load.start()
 
     def fill(dest, slot, buf):
         base = (dest // per_half) * wide + (dest % per_half) * own
@@ -198,8 +208,9 @@
             jnp.where(real, pltpu.roll(even, nvec, 1), odd),
         )
 
-    loads[1].wait()
-    loads[2].wait()
+    pairs = ((1, 2), (0, 2), (0, 1))
+    mat_load.wait()
+    shift_load.wait()
     for s in range(combos):
         for q in range(3):
             board[...] = mats_ref[spin_ref[s, q]]
@@ -210,23 +221,26 @@
             far = spin_mats[s, q, pl.ds(pl.multiple_of(other_side * half, half), half), :]
             local = jnp.concatenate([near, far], axis=0)
             local_mats[s, q] = local
-            at = (s * 3 + q) * lanes
-            top_hi, top_lo = halves(local)
-            low_hi, low_lo = halves(minus_plus * pltpu.roll(local, nvec, 1))
-            right_hh[0:nvec, at:at + lanes] = top_hi
-            right_hh[nvec:lanes, at:at + lanes] = low_hi
-            right_hh[lanes:lanes + nvec, at:at + lanes] = top_hi
-            right_hh[lanes + nvec:2 * lanes, at:at + lanes] = low_hi
-            right_lo[0:nvec, at:at + lanes] = top_lo
-            right_lo[nvec:lanes, at:at + lanes] = low_lo
-    pairs = ((1, 2), (0, 2), (0, 1))
-    for s in range(combos):
-        for p in range(3):
-            q, r = pairs[p]
-            both = jnp.transpose(jnp.concatenate([local_mats[s, q], local_mats[s, r]], axis=0))
-            hi, lo = halves(both)
-            left_hl[s * 3 + p, :, 0:lanes] = hi
-            left_hl[s * 3 + p, :, lanes:2 * lanes] = lo
+            parts = halves(local) + halves(minus_plus * pltpu.roll(local, nvec, 1))
+            for p in range(3):
+                if q in pairs[p]:
+                    at = pairs[p].index(q) * lanes
+                    for row, top, low_part in ((0, parts[0], parts[2]), (lanes, parts[1], parts[3])):
+                        right_hl[s * 3 + p, at:at + nvec, row:row + lanes] = top
+                        right_hl[s * 3 + p, at + nvec:at + lanes, row:row + lanes] = low_part
+    flat = [(s, q) for s in range(combos) for q in range(3)]
+    wide_real = lax.broadcasted_iota(jnp.int32, (nvec, lanes), 1) < nvec
+    for m in range(0, len(flat), 2):
+        ahead = flat[m + 1] if m + 1 < len(flat) else flat[m]
+        t = jnp.transpose(jnp.concatenate([local_mats[flat[m]], local_mats[ahead]], axis=0))
+        up, down = t[:nvec], t[nvec:]
+        here = jnp.where(wide_real, up, pltpu.roll(down, nvec, 1))
+        there = jnp.where(wide_real, pltpu.roll(up, nvec, 1), down)
+        for k, value in ((m, here), (m + 1, there)):
+            if k < len(flat):
+                hi, lo = halves(value)
+                left_hl[k * nvec:(k + 1) * nvec, 0:lanes] = hi
+                left_hl[k * nvec:(k + 1) * nvec, lanes:2 * lanes] = lo
     for s in range(combos):
         for p in range(3):
             if own % 8 == 0:
@@ -317,45 +331,55 @@
 
             top = around[a] - to_left(t[:half], t[nvec:nvec + half])
             bottom = -to_left(t[half:nvec], t[nvec + half:])
-            hi, lo = halves(jnp.concatenate([top, bottom], axis=0))
-            dense_hl[a * nvec:(a + 1) * nvec, 0:lanes] = hi
-            dense_hl[a * nvec:(a + 1) * nvec, lanes:2 * lanes] = lo
-
-    for s in range(combos):
-        at = s * 3 * lanes
-        got = dot(dense_hl[...], right_hh[:, at:at + 3 * lanes]) + dot(
-            dense_hl[:, 0:lanes], right_lo[:, at:at + 3 * lanes]
-        )
-        hi, lo = halves(got)
-        for q in range(3):
-            for a in range(own):
-                where = (s * 3 + q, slice(None), pl.ds(a * lanes, lanes))
-                half_hi[where] = hi[a * nvec:(a + 1) * nvec, q * lanes:(q + 1) * lanes]
-                half_lo[where] = lo[a * nvec:(a + 1) * nvec, q * lanes:(q + 1) * lanes]
+            value = jnp.concatenate([top, bottom], axis=0)
+            hi, lo = halves(value)
+            low_hi, low_lo = halves(minus_plus * pltpu.roll(value, nvec, 1))
+            at = pl.ds(a * lanes, lanes)
+            for start in (0, lanes):
+                dense_hh[start:start + nvec, at] = hi
+                dense_hh[start + nvec:start + lanes, at] = low_hi
+            dense_lo[0:nvec, at] = lo
+            dense_lo[nvec:lanes, at] = low_lo
+
+    mats_count = combos * 3
+    for a in range(0, own, 2):
+        at = pl.ds(a * lanes, 2 * lanes)
+        got = dot(left_hl[...], dense_hh[:, at]) + dot(left_hl[:, 0:lanes], dense_lo[:, at])
+        for b in range(2):
+            inner_ref[pl.ds(a + b, mats_count * nvec, stride=own), :] = got[:, b * lanes:(b + 1) * lanes]
+    rows = nvec * own
+    for m in range(mats_count):
+        hi, lo = halves(inner_ref[m * rows:(m + 1) * rows, :])
+        inner_hi[m * rows:(m + 1) * rows, :] = hi
+        inner_lo[m * rows:(m + 1) * rows, :] = lo
+    for r in range(1, chips):
+        own_copy(r).wait_recv()
+        forward(r).start()
+    near_lane = lax.broadcasted_iota(jnp.int32, (rows // 2, lanes), 1) % nvec < half
     for s in range(combos):
         for p in range(3):
             q, r = pairs[p]
             m = s * 3 + p
-            r_hi = jnp.concatenate([half_hi[s * 3 + r], half_hi[s * 3 + q]], axis=0)
-            r_lo = jnp.concatenate([half_lo[s * 3 + r], half_lo[s * 3 + q]], axis=0)
-            got = dot(left_hl[m], jnp.concatenate([r_hi, r_hi], axis=0)) + dot(
-                left_hl[m, :, 0:lanes], r_lo
-            )
-            for a in range(own):
-                at = a * lanes
-                whole = got[:nvec, at:at + lanes] + minus_plus * pltpu.roll(
-                    got[nvec:, at:at + lanes], nvec, 1
-                )
-                rows = pl.ds((m * own + a) * half, half)
-                cross_w[rows, :] = jnp.where(left, whole[half:], whole[:half])
-                same_w[rows, :] = -0.5 * jnp.where(left, whole[:half], whole[half:])
-    for r in range(1, chips):
-        own_copy(r).wait_recv()
-        forward(r).start()
+            at_q = pl.ds((s * 3 + q) * rows, rows)
+            at_r = pl.ds((s * 3 + r) * rows, rows)
+            left_hi = jnp.concatenate([inner_hi[at_r, :], inner_hi[at_q, :]], axis=1)
+            left_lo = jnp.concatenate([inner_lo[at_r, :], inner_lo[at_q, :]], axis=1)
+            both = dot(left_hi, right_hl[m])
+            whole = both[:, :lanes] + (both[:, lanes:] + dot(left_lo, right_hl[m, :, 0:lanes]))
+            up, down = whole[:rows // 2], whole[rows // 2:]
+            at = pl.ds(m * (rows // 2), rows // 2)
+            cross_w[at, :] = jnp.where(near_lane, down, up)
+            same_w[at, :] = -0.5 * jnp.where(near_lane, up, down)
+
+    def at_row(ref, k):
+        return jnp.concatenate(
+            [ref[(m * half + k) * own:(m * half + k + 1) * own, :] for m in range(mats_count)], axis=0
+        )
+
     c_real = lax.broadcasted_iota(jnp.int32, (count, lanes), 1) < nvec
     for m in range(half // 2):
-        even = same_w[pl.ds(2 * m, count, stride=half), :]
-        odd = same_w[pl.ds(2 * m + 1, count, stride=half), :]
+        even = at_row(same_w, 2 * m)
+        odd = at_row(same_w, 2 * m + 1)
         re = jnp.where(c_real, even, pltpu.roll(odd, nvec, 1))
         im = jnp.where(c_real, pltpu.roll(even, nvec, 1), odd)
         at = pl.ds(m * lanes, lanes)
@@ -403,18 +427,19 @@
                 parts.append(slab)
             slab = jnp.concatenate(parts, axis=0)
             hi, lo = halves(slab)
-            sl_hi[k * nvec:(k + 1) * nvec, :] = hi
-            sl_lo[k * nvec:(k + 1) * nvec, :] = lo
+            sl_hl[k * nvec:(k + 1) * nvec, 0:lanes] = hi
+            sl_hl[k * nvec:(k + 1) * nvec, lanes:2 * lanes] = lo
             m_hi, m_lo = halves(jnp.where(crossing, slab, 0.0))
             pair.append(jnp.concatenate([m_hi, m_lo, m_hi], axis=0))
         got = dot(mid_k, jnp.concatenate(pair, axis=1))
         for b, k in enumerate((y, y + 1)):
             here = got[:, b * lanes:(b + 1) * lanes]
             value = here[:count] + c_sign * pltpu.roll(here[low:low + count], nvec, 1)
-            weight = cross_w[pl.ds(k, count, stride=half), :]
+            weight = at_row(cross_w, k)
             one = one + value * weight
             two = two + value * pltpu.roll(weight, nvec, 1)
-    got = dot(lc_hi[...], sl_hi[...]) + (dot(lc_hi[...], sl_lo[...]) + dot(lc_lo[...], sl_hi[...]))
+    both = dot(lc_hi[...], sl_hl[...])
+    got = both[:, :lanes] + (both[:, lanes:] + dot(lc_lo[...], sl_hl[:, 0:lanes]))
     value = got[:count] + c_sign * pltpu.roll(got[low:low + count], nvec, 1)
     one = one + value * mid
     two = two + value * turned
@@ -541,7 +566,7 @@
             pltpu.VMEM(vec.shape, f32),
             pltpu.VMEM(mats.shape, f32),
             pltpu.SMEM(shift_steps.shape, jnp.int32),
-            dma((3,)),
+            dma((8,)),
             pltpu.VMEM((2, 3, sites // 128, 4 * wide, 128), f32),
             pltpu.VMEM((4 * nvec, 6 * sites), bf16),
             pltpu.VMEM((2, 2 * share, 6 * sites), bf16),
@@ -556,21 +581,21 @@
             pltpu.VMEM((nvec, lanes), f32),
             pltpu.VMEM((combos, 3, nvec, lanes), f32),
             pltpu.VMEM((combos, 3, nvec, lanes), f32),
-            pltpu.VMEM((2 * lanes, combos * 3 * lanes), bf16),
-            pltpu.VMEM((lanes, combos * 3 * lanes), bf16),
-            pltpu.VMEM((combos * 3, lanes, 2 * lanes), bf16),
+            pltpu.VMEM((combos * 3, 2 * lanes, 2 * lanes), bf16),
+            pltpu.VMEM((combos * 3 * nvec, 2 * lanes), bf16),
             pltpu.VMEM((max(own, 2) * wide, lanes), f32),
-            pltpu.VMEM((own * nvec, 2 * lanes), bf16),
-            pltpu.VMEM((combos * 3, nvec, own * lanes), bf16),
-            pltpu.VMEM((combos * 3, nvec, own * lanes), bf16),
+            pltpu.VMEM((2 * lanes, own * lanes), bf16),
+            pltpu.VMEM((lanes, own * lanes), bf16),
+            pltpu.VMEM((combos * 3 * nvec * own, lanes), f32),
+            pltpu.VMEM((combos * 3 * nvec * own, lanes), bf16),
+            pltpu.VMEM((combos * 3 * nvec * own, lanes), bf16),
             pltpu.VMEM((count * half, lanes), f32),
             pltpu.VMEM((count * half, lanes), f32),
             pltpu.VMEM((2 * low, half * nvec), bf16),
             pltpu.VMEM((2 * low, half * nvec), bf16),
             pltpu.VMEM((count, lanes), f32),
             pltpu.VMEM((nvec, half, lanes), f32),
-            pltpu.VMEM((half * nvec, lanes), bf16),
-            pltpu.VMEM((half * nvec, lanes), bf16),
+            pltpu.VMEM((half * nvec, 2 * lanes), bf16),
             pltpu.VMEM((lanes, lanes), f32),
             pltpu.VMEM((2, own * (nvec // 8), lanes), f32),
             pltpu.VMEM((2 * combos, lanes), f32),

time: 34.6 us -> 32.1 us (0.928)
  Pallas kernels: 31.9 us -> 29.4 us
    pallas_call x1, Pallas kernels: 31.9 us -> 29.4 us  [shards(): pl.pallas_call(functools.partial(elementals_kernel, n, times, scale, corr...]
where the time goes in v3:
time: 32.1 us; the launch traced here: 31.9 us
  Pallas kernels  29.4 us (92%)
  between operations  1.28 us (4%)
  local copies, waits for them, and re-layouts  1.27 us (4%)
    pallas_call x1, Pallas kernels, shards(): pl.pallas_call(functools.partial(elementals_kernel, n, times, scale, corr...  29.4 us
    unnamed x2, local copies, waits for them, and re-layouts  1.27 us

profile of v3, /device:TPU:0, one launch (start us, length us, event | category | flops | bytes accessed | tf_op | source)
XLA Modules:
  0.0 31.9 jit_solution(9140211807385773212)
XLA Ops:
  1.3 29.4 %elementals.1 = (f32[8,64,128]{2,1,0:T(8,128)S(1)}, f32[2,4]{1,0:T(2,128)S(1)}) custom-call(f32[2,3,64,256]{3,2,1,0:T(8,128)} %bitcast.17, f32[16,64,128]{2,1,0:T(8,128)} %bitcast.16, s32[1]{0:T(128)S(6)} %copy.12.shift_hbm, s32[4,3]{1,0:T(4,128)} %spin_ref.1), custom_call_target="tpu_custom_call" | custom-call | tf_op jit(solution)/shard_map/elementals/pallas_call | solution.py:557
  30.7 0.7 %copy.10 = f32[1,8,2,4096]{3,2,1,0:T(2,128)} copy(f32[1,8,2,4096]{3,2,1,0:T(2,128)S(1)} %bitcast.14) | data formatting | bytes 524288
  31.4 0.6 %copy.11 = f32[1,4,2]{1,2,0:T(2,128)} copy(f32[1,4,2]{1,2,0:T(2,128)S(1)} %bitcast.15) | data formatting | bytes 64

commit v4 on v3

--- a/solution.py
+++ b/solution.py
@@ -26,11 +26,11 @@
     n, times, scale, corr_scale, v_hbm, mats_hbm, shift_hbm, spin_ref, out_ref, corr_ref,
     v_ref, mats_ref, shift_ref, in_sem, vv, lead, d_hi, d_lo, keep, give, pair_in, chip_in, own_ref, full, sink_ref,
     board, spin_mats, local_mats, right_hl, left_hl, placed, dense_hh, dense_lo,
-    inner_ref, inner_hi, inner_lo, cross_w, same_w, lc_hi, lc_lo, mid_ref, slabs, sl_hl,
+    inner_ref, cross_w, same_w, lc_hi, lc_lo, mid_ref, slabs, sl_hl,
     turn, pick, tile_ref, box,
     pair_send, pair_recv, chip_send, chip_recv,
     own_send, own_recv, fwd_send, fwd_recv, tm_send, tm_recv,
-    sum_send, sum_recv,
+    sum_send, sum_recv, through_in, through_send, through_recv,
 ):
     f32 = jnp.float32
     me = lax.axis_index("space")
@@ -153,17 +153,27 @@
             device_id=(tm, partner(chips - 1 - s) * 2 + core), device_id_type=MESH,
         )
 
-    def fills(s, buf):
-        target = partner(chips - 1 - s) * 2
-        fill(target + 1 - core, 0, buf)
-        fill(target + core, 1, buf)
-
-    def products(s, buf):
-        both = lax.dot_general(d_hi[buf], lead[...], NT_DIMS, preferred_element_type=f32)
-        rest = lax.dot_general(d_lo[buf], lead[0:lanes], NT_DIMS, preferred_element_type=f32)
+    def fills(group, buf):
+        for slot, (part, s) in enumerate(group):
+            fill(partner(chips - 1 - s) * 2 + (1 - core if part == 0 else core), slot, buf)
+
+    def products(group, buf):
+        at = pl.ds(0, len(group) * share)
+        both = lax.dot_general(d_hi[buf, at, :], lead[...], NT_DIMS, preferred_element_type=f32)
+        rest = lax.dot_general(d_lo[buf, at, :], lead[0:lanes], NT_DIMS, preferred_element_type=f32)
         got = both[:, :lanes] + (both[:, lanes:] + rest)
-        give[s] = got[:share]
-        keep[s] = got[share:]
+        for slot, (part, s) in enumerate(group):
+            (give, keep)[part][s] = got[slot * share:(slot + 1) * share]
+
+    def add_pair(s):
+        pair_copy(s).wait_recv()
+        keep[s] = keep[s] + pair_in[s]
+
+    outer = chip % 3 == 0
+    through = pltpu.make_async_remote_copy(
+        keep.at[0], through_in, through_send, through_recv,
+        device_id=(tm, partner(1) * 2 + core), device_id_type=MESH,
+    )
 
     def relay(s):
         pair_copy(s).wait_recv()
@@ -171,28 +181,50 @@
         chip_copy(s).start()
 
     def one_chip(s, carry):
-        fills(s, 0)
-        products(s, 0)
+        for part in range(2):
+            fill(partner(chips - 1 - s) * 2 + (1 - core if part == 0 else core), part, 0)
+        both = lax.dot_general(d_hi[0], lead[...], NT_DIMS, preferred_element_type=f32)
+        rest = lax.dot_general(d_lo[0], lead[0:lanes], NT_DIMS, preferred_element_type=f32)
+        got = both[:, :lanes] + (both[:, lanes:] + rest)
+        give[s] = got[:share]
+        keep[s] = got[share:]
         pair_copy(s).start()
-        relay(s - 1)
+
+        @pl.when(s > 0)
+        def _():
+            relay(s - 1)
+
         return carry
 
-    fills(0, 0)
-    if chips <= 4:
-        for s in range(chips):
-            products(s, s % 2)
-            if s < chips - 1:
-                fills(s + 1, (s + 1) % 2)
-            if s == 0:
+    if chips == 4:
+        groups = (((0, 0),), ((0, 1), (0, 2)), ((1, 0), (0, 3)), ((1, 1), (1, 2)), ((1, 3),))
+        fills(groups[0], 0)
+        for k, group in enumerate(groups):
+            products(group, k % 2)
+            if k + 1 < len(groups):
+                fills(groups[k + 1], (k + 1) % 2)
+            if k == 0:
                 pl.semaphore_wait(barrier, n - 1 + times - 1)
-            pair_copy(s).start()
-            if s:
-                relay(s - 1)
+            for part, s in group:
+                if part == 0:
+                    pair_copy(s).start()
+            if k == 2:
+                add_pair(0)
+                pl.when(outer)(through.start)
+                pl.when(jnp.logical_not(outer))(chip_copy(0).start)
+        add_pair(1)
+        pl.when(outer)(chip_copy(1).start)
+        relay(2)
+
+        @pl.when(jnp.logical_not(outer))
+        def _():
+            through.wait_recv()
+            keep[1] = keep[1] + through_in[...]
+            chip_copy(1).start()
+
     else:
-        products(0, 0)
         pl.semaphore_wait(barrier, n - 1 + times - 1)
-        pair_copy(0).start()
-        lax.fori_loop(1, chips, one_chip, 0)
+        lax.fori_loop(0, chips, one_chip, 0)
 
     lane = lax.broadcasted_iota(jnp.int32, (half, lanes), 1)
     spot = lane % nvec
@@ -254,10 +286,21 @@
     last = chips - 1
     pair_copy(last).wait_recv()
     total = keep[last] + pair_in[last]
-    for s in range(last):
-        chip_copy(s).wait_recv()
-        total = total + chip_in[s]
-    own_ref[...] = total * scale
+    if chips == 4:
+        for s in (1, 2):
+            chip_copy(s).wait_recv()
+            total = total + chip_in[s]
+        own_ref[...] = total * scale
+
+        @pl.when(jnp.logical_not(outer))
+        def _():
+            chip_copy(0).wait_recv()
+            own_ref[...] = (total + chip_in[0]) * scale
+    else:
+        for s in range(last):
+            chip_copy(s).wait_recv()
+            total = total + chip_in[s]
+        own_ref[...] = total * scale
 
     def rows_of(d):
         start = (d // per_half) * block_rows + reach * reach + (d % per_half) * share
@@ -348,10 +391,6 @@
         for b in range(2):
             inner_ref[pl.ds(a + b, mats_count * nvec, stride=own), :] = got[:, b * lanes:(b + 1) * lanes]
     rows = nvec * own
-    for m in range(mats_count):
-        hi, lo = halves(inner_ref[m * rows:(m + 1) * rows, :])
-        inner_hi[m * rows:(m + 1) * rows, :] = hi
-        inner_lo[m * rows:(m + 1) * rows, :] = lo
     for r in range(1, chips):
         own_copy(r).wait_recv()
         forward(r).start()
@@ -362,8 +401,7 @@
             m = s * 3 + p
             at_q = pl.ds((s * 3 + q) * rows, rows)
             at_r = pl.ds((s * 3 + r) * rows, rows)
-            left_hi = jnp.concatenate([inner_hi[at_r, :], inner_hi[at_q, :]], axis=1)
-            left_lo = jnp.concatenate([inner_lo[at_r, :], inner_lo[at_q, :]], axis=1)
+            left_hi, left_lo = halves(jnp.concatenate([inner_ref[at_r, :], inner_ref[at_q, :]], axis=1))
             both = dot(left_hi, right_hl[m])
             whole = both[:, :lanes] + (both[:, lanes:] + dot(left_lo, right_hl[m, :, 0:lanes]))
             up, down = whole[:rows // 2], whole[rows // 2:]
@@ -410,6 +448,7 @@
     mid_k = jnp.concatenate([mid_hi, mid_hi, mid_lo], axis=1)
     one = jnp.zeros((count, lanes), f32)
     two = jnp.zeros((count, lanes), f32)
+    got_same = None
     for y in range(0, half, 2):
         pair = []
         for k in (y, y + 1):
@@ -438,8 +477,12 @@
             weight = at_row(cross_w, k)
             one = one + value * weight
             two = two + value * pltpu.roll(weight, nvec, 1)
-    both = dot(lc_hi[...], sl_hl[...])
-    got = both[:, :lanes] + (both[:, lanes:] + dot(lc_lo[...], sl_hl[:, 0:lanes]))
+        if (y + 2) % (half // 4) == 0:
+            at = pl.ds((y + 2 - half // 4) * nvec, half // 4 * nvec)
+            both = dot(lc_hi[:, at], sl_hl[at, :])
+            both = both[:, :lanes] + (both[:, lanes:] + dot(lc_lo[:, at], sl_hl[at, 0:lanes]))
+            got_same = both if got_same is None else got_same + both
+    got = got_same
     value = got[:count] + c_sign * pltpu.roll(got[low:low + count], nvec, 1)
     one = one + value * mid
     two = two + value * turned
@@ -513,8 +556,14 @@
 
     for s in range(chips):
         pair_copy(s).wait_send()
-    for s in range(chips - 1):
-        chip_copy(s).wait_send()
+    if chips == 4:
+        pl.when(outer)(through.wait_send)
+        pl.when(jnp.logical_not(outer))(chip_copy(0).wait_send)
+        chip_copy(1).wait_send()
+        chip_copy(2).wait_send()
+    else:
+        for s in range(chips - 1):
+            chip_copy(s).wait_send()
     for r in range(1, times):
         tm_copy(r).wait_send()
     own_copy(0).wait_send()
@@ -587,8 +636,6 @@
             pltpu.VMEM((2 * lanes, own * lanes), bf16),
             pltpu.VMEM((lanes, own * lanes), bf16),
             pltpu.VMEM((combos * 3 * nvec * own, lanes), f32),
-            pltpu.VMEM((combos * 3 * nvec * own, lanes), bf16),
-            pltpu.VMEM((combos * 3 * nvec * own, lanes), bf16),
             pltpu.VMEM((count * half, lanes), f32),
             pltpu.VMEM((count * half, lanes), f32),
             pltpu.VMEM((2 * low, half * nvec), bf16),
@@ -606,6 +653,7 @@
             dma((chips - 1,)), dma((chips - 1,)),
             dma((times - 1,)), dma((times - 1,)),
             dma((n - 1,)), dma((n - 1,)),
+            pltpu.VMEM(tile, f32), dma, dma,
         ],
         compiler_params=pltpu.CompilerParams(
             collective_id=0, has_side_effects=True, vmem_limit_bytes=60 * 1024 * 1024

time: 32.1 us -> 31.5 us (0.981)
  Pallas kernels: 29.4 us -> 28.7 us
    pallas_call x1, Pallas kernels: 29.4 us -> 28.7 us  [shards(): pl.pallas_call(functools.partial(elementals_kernel, n, times, scale, corr...]
where the time goes in v4:
time: 31.5 us; the launch traced here: 31.3 us
  Pallas kernels  28.7 us (91%)
  between operations  1.28 us (4%)
  local copies, waits for them, and re-layouts  1.27 us (4%)
    pallas_call x1, Pallas kernels, shards(): pl.pallas_call(functools.partial(elementals_kernel, n, times, scale, corr...  28.7 us
    unnamed x2, local copies, waits for them, and re-layouts  1.27 us

profile of v4, /device:TPU:0, one launch (start us, length us, event | category | flops | bytes accessed | tf_op | source)
XLA Modules:
  0.0 31.3 jit_solution(864190277339901241)
XLA Ops:
  1.3 28.7 %elementals.1 = (f32[8,64,128]{2,1,0:T(8,128)S(1)}, f32[2,4]{1,0:T(2,128)S(1)}) custom-call(f32[2,3,64,256]{3,2,1,0:T(8,128)} %bitcast.17, f32[16,64,128]{2,1,0:T(8,128)} %bitcast.16, s32[1]{0:T(128)S(6)} %copy.12.shift_hbm, s32[4,3]{1,0:T(4,128)} %spin_ref.1), custom_call_target="tpu_custom_call" | custom-call | tf_op jit(solution)/shard_map/elementals/pallas_call | solution.py:606
  30.0 0.7 %copy.10 = f32[1,8,2,4096]{3,2,1,0:T(2,128)} copy(f32[1,8,2,4096]{3,2,1,0:T(2,128)S(1)} %bitcast.14) | data formatting | bytes 524288
  30.7 0.6 %copy.11 = f32[1,4,2]{1,2,0:T(2,128)} copy(f32[1,4,2]{1,2,0:T(2,128)S(1)} %bitcast.15) | data formatting | bytes 64

commit v5 on v4

--- a/solution.py
+++ b/solution.py
@@ -197,7 +197,7 @@
         return carry
 
     if chips == 4:
-        groups = (((0, 0),), ((0, 1), (0, 2)), ((1, 0), (0, 3)), ((1, 1), (1, 2)), ((1, 3),))
+        groups = (((0, 0),), ((0, 1), (0, 2)), ((1, 0),), ((1, 1), (1, 2)), ((0, 3), (1, 3)))
         fills(groups[0], 0)
         for k, group in enumerate(groups):
             products(group, k % 2)
@@ -394,6 +394,26 @@
     for r in range(1, chips):
         own_copy(r).wait_recv()
         forward(r).start()
+    def at_row(ref, k, some):
+        return jnp.concatenate(
+            [ref[(m * half + k) * own:(m * half + k + 1) * own, :] for m in some], axis=0
+        )
+
+    def pack(some):
+        begin, size = some[0] * own, len(some) * own
+        first_lanes = lax.broadcasted_iota(jnp.int32, (size, lanes), 1) < nvec
+        for m in range(half // 2):
+            even = at_row(same_w, 2 * m, some)
+            odd = at_row(same_w, 2 * m + 1, some)
+            re = jnp.where(first_lanes, even, pltpu.roll(odd, nvec, 1))
+            im = jnp.where(first_lanes, pltpu.roll(even, nvec, 1), odd)
+            at = pl.ds(m * lanes, lanes)
+            for start, value in ((begin, re), (low + begin, im)):
+                hi, lo = halves(value)
+                lc_hi[start:start + size, at] = hi
+                lc_lo[start:start + size, at] = lo
+
+    parts_of = 2 if combos % 2 == 0 and count // 2 % 16 == 0 else 1
     near_lane = lax.broadcasted_iota(jnp.int32, (rows // 2, lanes), 1) % nvec < half
     for s in range(combos):
         for p in range(3):
@@ -408,24 +428,11 @@
             at = pl.ds(m * (rows // 2), rows // 2)
             cross_w[at, :] = jnp.where(near_lane, down, up)
             same_w[at, :] = -0.5 * jnp.where(near_lane, up, down)
-
-    def at_row(ref, k):
-        return jnp.concatenate(
-            [ref[(m * half + k) * own:(m * half + k + 1) * own, :] for m in range(mats_count)], axis=0
-        )
+        if (s + 1) % (combos // parts_of) == 0:
+            done = mats_count // parts_of
+            pack(range((s + 1) * 3 - done, (s + 1) * 3))
 
     c_real = lax.broadcasted_iota(jnp.int32, (count, lanes), 1) < nvec
-    for m in range(half // 2):
-        even = at_row(same_w, 2 * m)
-        odd = at_row(same_w, 2 * m + 1)
-        re = jnp.where(c_real, even, pltpu.roll(odd, nvec, 1))
-        im = jnp.where(c_real, pltpu.roll(even, nvec, 1), odd)
-        at = pl.ds(m * lanes, lanes)
-        for start, value in ((0, re), (low, im)):
-            hi, lo = halves(value)
-            lc_hi[start:start + count, at] = hi
-            lc_lo[start:start + count, at] = lo
-
     own_copy(0).wait_recv()
     for r in range(1, chips):
         forward(r).wait_recv()
@@ -474,7 +481,7 @@
         for b, k in enumerate((y, y + 1)):
             here = got[:, b * lanes:(b + 1) * lanes]
             value = here[:count] + c_sign * pltpu.roll(here[low:low + count], nvec, 1)
-            weight = at_row(cross_w, k)
+            weight = at_row(cross_w, k, range(mats_count))
             one = one + value * weight
             two = two + value * pltpu.roll(weight, nvec, 1)
         if (y + 2) % (half // 4) == 0:

time: 31.5 us -> 31.2 us (level)
  no operation moved by 1% of the time
where the time goes in v5:
time: 31.2 us; the launch traced here: 31 us
  Pallas kernels  28.5 us (91%)
  between operations  1.28 us (4%)
  local copies, waits for them, and re-layouts  1.27 us (4%)
    pallas_call x1, Pallas kernels, shards(): pl.pallas_call(functools.partial(elementals_kernel, n, times, scale, corr...  28.5 us
    unnamed x2, local copies, waits for them, and re-layouts  1.27 us

profile of v5, /device:TPU:0, one launch (start us, length us, event | category | flops | bytes accessed | tf_op | source)
XLA Modules:
  0.0 31.0 jit_solution(3193439363737725196)
XLA Ops:
  1.3 28.5 %elementals.1 = (f32[8,64,128]{2,1,0:T(8,128)S(1)}, f32[2,4]{1,0:T(2,128)S(1)}) custom-call(f32[2,3,64,256]{3,2,1,0:T(8,128)} %bitcast.17, f32[16,64,128]{2,1,0:T(8,128)} %bitcast.16, s32[1]{0:T(128)S(6)} %copy.12.shift_hbm, s32[4,3]{1,0:T(4,128)} %spin_ref.1), custom_call_target="tpu_custom_call" | custom-call | tf_op jit(solution)/shard_map/elementals/pallas_call | solution.py:613
  29.7 0.7 %copy.10 = f32[1,8,2,4096]{3,2,1,0:T(2,128)} copy(f32[1,8,2,4096]{3,2,1,0:T(2,128)S(1)} %bitcast.14) | data formatting | bytes 524288
  30.5 0.6 %copy.11 = f32[1,4,2]{1,2,0:T(2,128)} copy(f32[1,4,2]{1,2,0:T(2,128)S(1)} %bitcast.15) | data formatting | bytes 64
